TPU v7x, 128 devices: a whole 4x4x4 slice. The times are simulated.
128 devices in a mesh: box: 64 (over z, y, x), col: 2 (over core).
Axes of the slice: x: 4, y: 4, z: 4, core: 2. Of those that a mesh axis runs over, the one named last changes fastest.
Arguments:
- points: bfloat16 [1024, 3, 512], P('box'), may hold values from 0 to 1
- sketch: bfloat16 [1024, 512, 128], P('box', 'col'), may hold values from -6 to 6
- near_mask: int32 [1024, 9], P('box'), may hold values from 0 to 1, as said below
Outputs:
- basis: bfloat16 [1024, 512, 128], P('box', 'col')
- coupling: float32 [1024, 9, 128, 128], P('box', None, 'col')
Inputs may be any that keep to these rules, and one draw needn't show every extreme that they name: near_mask[b, s] is 1 for the box itself and for its edge neighbours that lie on the plate, 0 for slots off the plate; a diagonal neighbour is near or not by a relation that is symmetric between the two boxes.
All inputs are finite; a program needn't handle non-finite values.
Results may differ from a plain program's by a relative error of at most 0.007.
Values may be sent and summed in bfloat16 or wider, within the bound.
A program may use at most 64 MiB of HBM per device.

v0:
```python
import math

import jax
import jax.numpy as jnp
from jax import lax
from jax.sharding import PartitionSpec as P

lift_scale = 0.25


def shortened(array):

    def short(part):
        return part.astype(jnp.bfloat16) if part.dtype == jnp.float32 else part

    return jax.tree.map(short, array)


def from_behind(value, axis, steps):
    count = lax.axis_size(axis)
    initial, last = (max(0, -steps), min(count, count - steps))
    return lax.ppermute(value, axis, [(source, source + steps) for source in range(initial, last)])


def interaction(row_points, col_points, shift_y, shift_x, first_row, first_col, centre, box_points):
    row_coords = row_points.astype(jnp.float32)
    col_coords = col_points.astype(jnp.float32)
    delta_u = shift_x + col_coords[..., 0, None, :] - row_coords[..., 0, :, None]
    delta_v = shift_y + col_coords[..., 1, None, :] - row_coords[..., 1, :, None]
    delta_w = lift_scale * (col_coords[..., 2, None, :] - row_coords[..., 2, :, None])
    strength = 0.25 / math.sqrt(box_points)
    soften = 0.5 / math.sqrt(box_points)
    values = strength / jnp.sqrt(
        delta_u * delta_u + delta_v * delta_v + delta_w * delta_w + soften * soften
    )
    if centre:
        row_ids = first_row + jnp.arange(row_coords.shape[-1], dtype=jnp.int32)
        col_ids = first_col + jnp.arange(col_coords.shape[-1], dtype=jnp.int32)
        values = values + jnp.where(row_ids[:, None] == col_ids[None, :], 1.0, 0.0).astype(
            jnp.float32
        )
    return values


def facing(offset, tile_side):
    if offset == -1:
        return slice(tile_side - 1, tile_side)
    if offset == 1:
        return slice(0, 1)
    return slice(0, tile_side)


def landing(offset, tile_side):
    if offset == -1:
        return slice(0, 1)
    if offset == 1:
        return slice(tile_side + 1, tile_side + 2)
    return slice(1, tile_side + 1)


def neighbours(arrays, tile_side, grid_side):
    extended = [
        jnp.zeros((tile_side + 2, tile_side + 2) + member.shape[2:], member.dtype)
        .at[1 : tile_side + 1, 1 : tile_side + 1]
        .set(member)
        for member in arrays
    ]
    for offset_y in (-1, 0, 1):
        for offset_x in (-1, 0, 1):
            if offset_y == 0 and offset_x == 0:
                continue
            pieces = tuple(
                (
                    member[facing(offset_y, tile_side), facing(offset_x, tile_side)]
                    for member in arrays
                )
            )
            received = jax.tree.map(
                lambda part, own: part.astype(own.dtype),
                from_behind(shortened(pieces), "box", -(offset_y * grid_side + offset_x)),
                pieces,
            )
            extended = [
                holder.at[landing(offset_y, tile_side), landing(offset_x, tile_side)].set(arrived)
                for holder, arrived in zip(extended, received)
            ]
    return extended


def slot_view(extended, row_index, offset_y, offset_x, tile_side):
    row_block = lax.dynamic_index_in_dim(extended, row_index + 1 + offset_y, 0, keepdims=False)
    return row_block[1 + offset_x : 1 + offset_x + tile_side]


def apply_inverse(gram_sum, sketch_t):
    lower_factor = jnp.linalg.cholesky(gram_sum)
    identity = jnp.broadcast_to(jnp.eye(gram_sum.shape[1], dtype=gram_sum.dtype), gram_sum.shape)
    inverse_lower = lax.linalg.triangular_solve(lower_factor, identity, left_side=True, lower=True)
    return jnp.einsum("brs,bsm->brm", inverse_lower, sketch_t, precision=lax.Precision.HIGHEST)


def orthonormal(sketch_t, box_points):
    gram_sum = (
        jnp.einsum("brm,bsm->brs", sketch_t, sketch_t, precision=lax.Precision.HIGHEST) / box_points
    )
    gram_sum = lax.psum(gram_sum, "col")
    return apply_inverse(gram_sum, sketch_t)


def body(points, sketch, near_mask):
    box_count = points.shape[0]
    tile_side = math.isqrt(box_count)
    grid_side = math.isqrt(lax.axis_size("box"))
    box_points = points.shape[2]
    half_points = sketch.shape[1]
    skel_rank = sketch.shape[2]
    col_index = lax.axis_index("col")
    own_start = col_index * half_points
    weights = near_mask.astype(jnp.float32).reshape(tile_side, tile_side, 9)
    coord_grid = points.reshape(tile_side, tile_side, 3, box_points)
    omega_grid = sketch.reshape(tile_side, tile_side, half_points, skel_rank)
    ext_coords, ext_omega = neighbours((coord_grid, omega_grid), tile_side, grid_side)
    tile_rows = jnp.arange(tile_side, dtype=jnp.int32)
    start = jnp.int32(0)
    rows_all = points.reshape(tile_side, tile_side, 3, half_points * lax.axis_size("col"))

    def sketch_row(row_index):
        row_coords = lax.dynamic_index_in_dim(rows_all, row_index, 0, keepdims=False)
        row_weights = lax.dynamic_index_in_dim(weights, row_index, 0, keepdims=False)
        running = jnp.zeros((half_points * lax.axis_size("col"), tile_side, skel_rank), jnp.float32)
        for stencil in range(9):
            offset_y = stencil // 3 - 1
            offset_x = stencil % 3 - 1
            near_coords = lax.dynamic_slice_in_dim(
                slot_view(ext_coords, row_index, offset_y, offset_x, tile_side),
                own_start,
                half_points,
                2,
            )
            near_omega = slot_view(ext_omega, row_index, offset_y, offset_x, tile_side)
            block_vals = interaction(
                row_coords,
                near_coords,
                offset_y,
                offset_x,
                start,
                own_start,
                stencil == 4,
                box_points,
            ).astype(jnp.bfloat16)
            running = (
                running
                + jnp.einsum(
                    "bij,bjr->ibr", block_vals, near_omega, preferred_element_type=jnp.float32
                )
                * row_weights[None, :, stencil, None]
            )
        return running

    blocks = lax.map(sketch_row, tile_rows)
    sketch_half = lax.psum_scatter(
        jnp.transpose(blocks, (1, 0, 2, 3)).reshape(
            half_points * lax.axis_size("col"), box_count * skel_rank
        ),
        "col",
        scatter_dimension=0,
        tiled=True,
    )
    sketch_t = jnp.transpose(sketch_half.reshape(half_points, box_count, skel_rank), (1, 2, 0))
    sketch_t = orthonormal(orthonormal(sketch_t, box_points), box_points)
    basis_t = sketch_t.astype(jnp.bfloat16)
    basis_out = jnp.transpose(basis_t, (0, 2, 1))
    ext_basis = neighbours(
        (basis_out.reshape(tile_side, tile_side, half_points, skel_rank),), tile_side, grid_side
    )[0]
    own_whole = lax.all_gather(basis_t, "col", axis=2, tiled=True).reshape(
        tile_side, tile_side, skel_rank, box_points
    )

    def couple_row(row_index):
        row_coords = lax.dynamic_index_in_dim(coord_grid, row_index, 0, keepdims=False)
        row_weights = lax.dynamic_index_in_dim(weights, row_index, 0, keepdims=False)
        own_basis = lax.dynamic_index_in_dim(own_whole, row_index, 0, keepdims=False)
        collected = []
        for stencil in range(9):
            offset_y = stencil // 3 - 1
            offset_x = stencil % 3 - 1
            near_coords = lax.dynamic_slice_in_dim(
                slot_view(ext_coords, row_index, offset_y, offset_x, tile_side),
                own_start,
                half_points,
                2,
            )
            near_basis = slot_view(ext_basis, row_index, offset_y, offset_x, tile_side)
            block_vals = interaction(
                row_coords, near_coords, offset_y, offset_x, 0, own_start, stencil == 4, box_points
            ).astype(jnp.bfloat16)
            projected = jnp.einsum(
                "bri,bij->brj", own_basis, block_vals, preferred_element_type=jnp.float32
            ).astype(jnp.bfloat16)
            coupling_term = (
                jnp.einsum(
                    "brj,bjs->brs", projected, near_basis, preferred_element_type=jnp.float32
                )
                * (1.0 / box_points)
                * row_weights[:, stencil, None, None]
            )
            collected.append(coupling_term)
        return jnp.stack(collected, axis=1)

    partials = lax.map(couple_row, tile_rows).reshape(box_count, 9, skel_rank, skel_rank)
    coupling = lax.psum_scatter(
        partials.astype(jnp.bfloat16), "col", scatter_dimension=2, tiled=True
    ).astype(jnp.float32)
    return (basis_out, coupling)


def solution(mesh):
    return jax.shard_map(
        body,
        mesh=mesh,
        in_specs=(P("box", None, None), P("box", "col", None), P("box", None)),
        out_specs=(P("box", "col", None), P("box", None, "col", None)),
        check_vma=False,
    )
```

profile of v0, /device:TPU:1, one launch (start us, length us, event | category | flops | bytes accessed | tf_op | source)
XLA Modules:
  0.0 1197.6 jit_solution(15406422334357513114)
XLA Ops:
  8.8 7.1 collective-permute-start.8
  16.7 3.3 collective-permute-start.9
  20.0 3.9 collective-permute-start.10
  24.6 4.0 collective-permute-start.11
  41.3 2.7 scatter.109
  45.3 9.5 collective-permute-start
  54.8 5.8 collective-permute-start.1
  60.5 2.5 broadcast_select_fusion
  63.1 2.6 scatter.110
  68.9 3.9 collective-permute-start.2
  74.2 4.0 collective-permute-start.3
  92.3 6.5 collective-permute-done.6
  98.9 2.4 copy.65
  101.3 97.2 %while.55 = (s32[]{:T(128)}, f32[4,512,4,128]{1,3,2,0:T(8,128)}, s32[4]{0:T(128)S(1)}, bf16[6,6,256,128]{2,3,1,0:T(8,128)(2,1)}, bf16[6,6,3,512]{3,1,2,0:T(8,128...) while((s32[]{:T(128)}, f32[4,512,4,128]{1,3,2,0:T(8,128)}, ...), condition=%wide.region_2.0_spmd, body=%wide.region_1.0_spmd.sunk | while | flops 1269871872 | bytes 31483436 | solution.py:160
  108.3 2.5 convolution_multiply_fusion.12
  132.6 2.5 convolution_multiply_fusion.12
  156.9 2.5 convolution_multiply_fusion.12
  181.2 2.5 convolution_multiply_fusion.12
  198.6 28.0 %reduce-scatter.3.cloned.1.call-done = f32[256,2048]{0,1:T(8,128)} async-done(((f32[512,2048]{0,1:T(8,128)}), f32[256,2048]{0,1:T(8,128)}) %reduce-scatter.3.cloned.1.call-update) | async-done | bytes 2097168 | tf_op jit(solution)/shard_map/reduce_scatter | solution.py:161
  226.6 5.3 convolution_multiply_fusion.10
  231.9 9.5 all-reduce.8.cloned.1.call-start
  241.5 17.0 %all-reduce.6.cloned.1.call-done = f32[16,128,128]{1,2,0:T(8,128)} async-done(((f32[16,128,128]{1,2,0:T(8,128)}), f32[16,128,128]{1,2,0:T(8,128)}) %all-reduce.6.cloned.1.call-update) | async-done | bytes 1048592 | tf_op jit(solution)/shard_map/psum | solution.py:106
  260.3 187.5 %custom-call.8 = f32[16,128,128]{2,1,0:T(8,128)S(1)} custom-call(f32[16,128,128]{2,1,0:T(8,128)S(1)} %fusion.487), custom_call_target="Cholesky" | custom-call | tf_op jit(solution)/shard_map/jit(cholesky)/cholesky | solution.py:96
  448.3 157.2 %custom-call.9 = f32[16,1,128,128]{2,3,1,0:T(8,128)S(1)} custom-call(f32[16,1,128,128]{3,2,1,0:T(8,128)S(1)} %select_bitcast_fusion.1), custom_call_target="InvertDiagBlocksLowerTriangular" | custom-call | tf_op jit(solution)/shard_map/triangular_solve/custom-call.0 | solution.py:98
  607.3 3.5 fusion.499
  610.8 3.1 convolution_multiply_fusion.9
  614.0 26.5 %all-reduce.8.cloned.1.call-done = f32[16,128,128]{1,2,0:T(8,128)} async-done(((f32[16,128,128]{1,2,0:T(8,128)}), f32[16,128,128]{1,2,0:T(8,128)}) %all-reduce.8.cloned.1.call-update) | async-done | bytes 1048592 | tf_op jit(solution)/shard_map/psum | solution.py:106
  640.4 2.6 copy.72
  645.3 188.7 %custom-call.10 = f32[16,128,128]{2,1,0:T(8,128)S(1)} custom-call(f32[16,128,128]{2,1,0:T(8,128)} %fusion.484), custom_call_target="Cholesky" | custom-call | tf_op jit(solution)/shard_map/jit(cholesky)/cholesky | solution.py:96
  835.4 157.9 %custom-call.11 = f32[16,1,128,128]{2,3,1,0:T(8,128)S(1)} custom-call(f32[16,1,128,128]{3,2,1,0:T(8,128)} %select_bitcast_fusion), custom_call_target="InvertDiagBlocksLowerTriangular" | custom-call | tf_op jit(solution)/shard_map/triangular_solve/custom-call.0 | solution.py:98
  995.2 2.9 convolution_convert_fusion.9
  1000.5 5.6 collective-permute-start.16
  1006.9 3.1 collective-permute-start.17
  1013.2 3.7 collective-permute-start.18
  1016.9 4.9 collective-permute-start.19
  1028.7 3.2 select_dynamic-update-slice_fusion
  1037.7 118.1 %while.56 = (s32[]{:T(128)}, bf16[4,4,9,128,128]{4,3,1,2,0:T(8,128)(2,1)}, s32[4]{0:T(128)S(1)}, bf16[4,4,128,512]{3,2,1,0:T(8,128)(2,1)}, bf16[6,6,3,512]{3,1,2...) while((s32[]{:T(128)}, ...), condition=%wide.region_9.12_spmd, body=%wide.region_8.11_spmd.sunk | while | flops 1569174784 | bytes 13657660 | solution.py:211
  1047.1 2.4 fusion.577
  1049.5 2.4 fusion.578
  1051.9 2.4 fusion.579
  1054.3 2.4 fusion.581
  1056.8 2.4 fusion.583
  1061.5 2.4 fusion.586
  1063.9 2.4 fusion.587
  1076.6 2.4 fusion.577
  1079.0 2.4 fusion.578
  1083.8 2.4 fusion.581
  1086.2 2.4 fusion.583
  1088.6 2.4 fusion.584
  1091.0 2.4 fusion.586
  1108.5 2.4 fusion.578
  1113.3 2.4 fusion.581
  1115.7 2.4 fusion.583
  1118.1 2.4 fusion.584
  1120.5 2.4 fusion.586
  1135.6 2.4 fusion.577
  1137.9 2.4 fusion.578
  1142.7 2.4 fusion.581
  1145.2 2.4 fusion.583
  1147.6 2.4 fusion.584
  1149.9 2.4 fusion.586
  1155.8 6.3 copy.85
  1163.4 23.2 %reduce-scatter.5.cloned.1.call-done = bf16[16,9,64,128]{3,2,1,0:T(8,128)(2,1)} async-done(((bf16[16,9,128,128]{3,2,1,0:T(8,128)(2,1)}), bf16[16,9,64,128]{3,2,1,0:T(8,128)(2,1)}) %reduce-scatter.5.cloned.1.call-update) | async-done | bytes 2359312 | tf_op jit(solution)/shard_map/reduce_scatter | solution.py:212
  1186.5 4.4 convert_element_type.530
  (281 shorter events, 166.0 us)
Async XLA Ops:
  7.2 27.6 %copy-start.6 = (s32[4]{0:T(128)S(1)}, s32[4]{0:T(128)}, u32[]{:S(2)}) copy-start(s32[4]{0:T(128)} %constant.1031.clone.1) | copy-start | bytes 52
  7.2 26.2 %copy-start.1 = (bf16[16,256,128]{2,1,0:T(8,128)(2,1)S(1)}, bf16[16,256,128]{2,1,0:T(8,128)(2,1)}, u32[]{:S(2)}) copy-start(bf16[16,256,128]{2,1,0:T(8,128)(2,1)} %param.65) | copy-start | bytes 3145732
  7.2 219.4 %reduce-scatter.3.cloned.1.call-start = ((), (), s32[]{:S(2)}) async-start(), calls=%async_computation.2 | async-start | bytes 6291456 | tf_op jit(solution)/shard_map/reduce_scatter | solution.py:161
  8.8 28.5 %collective-permute-start.8 = (bf16[1,1,3,512]{3,1,0,2:T(2,128)(2,1)}, bf16[1,1,3,512]{3,1,0,2:T(2,128)(2,1)}, u32[]{:S(2)}, u32[]{:S(2)}) collective-permute-start(bf16[1,1,3,512]{3,1,0,2:T(2,128)(2,1)} %get-tuple-element.934), channel_id=1, source_target_pairs={{0,18},{2,20},{4,22},{6,24},{8,26},{10,28},{12,30},{14,32},{16,34}... | collective-permute-start | bytes 9224 | tf_op jit(solution)/shard_map/ppermute | solution.py:22
  16.7 23.3 %collective-permute-start.9 = (bf16[1,4,3,512]{3,1,0,2:T(4,128)(2,1)S(1)}, bf16[1,4,3,512]{3,1,0,2:T(4,128)(2,1)S(1)}, u32[]{:S(2)}, u32[]{:S(2)}) collective-permute-start(bf16[1,4,3,512]{3,1,0,2:T(4,128)(2,1)S(1)} %get-tuple-element.936), channel_id=1, source_target_pairs={{0,16},{2,18},{4,20},{6,22},{8,24},{10,26},{12,28},{14,30},{16,32}... | collective-permute-start | bytes 36872 | tf_op jit(solution)/shard_map/ppermute | solution.py:22
  20.0 24.0 %collective-permute-start.10 = (bf16[1,1,3,512]{3,1,0,2:T(2,128)(2,1)}, bf16[1,1,3,512]{3,1,0,2:T(2,128)(2,1)}, u32[]{:S(2)}, u32[]{:S(2)}) collective-permute-start(bf16[1,1,3,512]{3,1,0,2:T(2,128)(2,1)} %get-tuple-element.933), channel_id=1, source_target_pairs={{0,14},{2,16},{4,18},{6,20},{8,22},{10,24},{12,26},{14,28},{16,30}... | collective-permute-start | bytes 9224 | tf_op jit(solution)/shard_map/ppermute | solution.py:22
  24.6 20.7 %collective-permute-start.11 = (bf16[4,1,3,512]{3,1,0,2:T(2,128)(2,1)S(1)}, bf16[4,1,3,512]{3,1,0,2:T(2,128)(2,1)S(1)}, u32[]{:S(2)}, u32[]{:S(2)}) collective-permute-start(bf16[4,1,3,512]{3,1,0,2:T(2,128)(2,1)S(1)} %get-tuple-element.938), channel_id=1, source_target_pairs={{0,2},{2,4},{4,6},{6,8},{8,10},{10,12},{12,14},{14,16},{16,18},{18... | collective-permute-start | bytes 36872 | tf_op jit(solution)/shard_map/ppermute | solution.py:22
  28.6 26.2 %collective-permute-start.12 = (bf16[4,1,3,512]{3,1,0,2:T(2,128)(2,1)}, bf16[4,1,3,512]{3,1,0,2:T(2,128)(2,1)}, u32[]{:S(2)}, u32[]{:S(2)}) collective-permute-start(bf16[4,1,3,512]{3,1,0,2:T(2,128)(2,1)} %get-tuple-element.937), channel_id=1, source_target_pairs={{2,0},{4,2},{6,4},{8,6},{10,8},{12,10},{14,12},{16,14},{18,16},{20... | collective-permute-start | bytes 36872 | tf_op jit(solution)/shard_map/ppermute | solution.py:22
  34.2 3.1 copy-start.5
  37.3 31.6 %collective-permute-start.13 = (bf16[1,1,3,512]{3,1,0,2:T(2,128)(2,1)}, bf16[1,1,3,512]{3,1,0,2:T(2,128)(2,1)S(1)}, u32[]{:S(2)}, u32[]{:S(2)}) collective-permute-start(bf16[1,1,3,512]{3,1,0,2:T(2,128)(2,1)} %get-tuple-element.932), channel_id=1, source_target_pairs={{14,0},{16,2},{18,4},{20,6},{22,8},{24,10},{26,12},{28,14},{30,16}... | collective-permute-start | bytes 9224 | tf_op jit(solution)/shard_map/ppermute | solution.py:22
  40.0 34.2 %collective-permute-start.14 = (bf16[1,4,3,512]{3,1,0,2:T(4,128)(2,1)S(1)}, bf16[1,4,3,512]{3,1,0,2:T(4,128)(2,1)S(1)}, u32[]{:S(2)}, u32[]{:S(2)}) collective-permute-start(bf16[1,4,3,512]{3,1,0,2:T(4,128)(2,1)S(1)} %get-tuple-element.935), channel_id=1, source_target_pairs={{16,0},{18,2},{20,4},{22,6},{24,8},{26,10},{28,12},{30,14},{32,16}... | collective-permute-start | bytes 36872 | tf_op jit(solution)/shard_map/ppermute | solution.py:22
  44.0 35.6 %collective-permute-start.15 = (bf16[1,1,3,512]{3,1,0,2:T(2,128)(2,1)}, bf16[1,1,3,512]{3,1,0,2:T(2,128)(2,1)S(1)}, u32[]{:S(2)}, u32[]{:S(2)}) collective-permute-start(bf16[1,1,3,512]{3,1,0,2:T(2,128)(2,1)} %get-tuple-element.931), channel_id=1, source_target_pairs={{18,0},{20,2},{22,4},{24,6},{26,8},{28,10},{30,12},{32,14},{34,16}... | collective-permute-start | bytes 9224 | tf_op jit(solution)/shard_map/ppermute | solution.py:22
  45.3 37.9 %collective-permute-start = (bf16[1,1,256,128]{3,2,1,0:T(8,128)(2,1)}, bf16[1,1,256,128]{3,2,1,0:T(8,128)(2,1)S(1)}, u32[]{:S(2)}, u32[]{:S(2)}) collective-permute-start(bf16[1,1,256,128]{3,2,1,0:T(8,128)(2,1)} %get-tuple-element.926), channel_id=1, source_target_pairs={{0,18},{2,20},{4,22},{6,24},{8,26},{10,28},{12,30},{14,32},{16,34}... | collective-permute-start | bytes 196616 | tf_op jit(solution)/shard_map/ppermute | solution.py:22
  54.8 29.8 %collective-permute-start.1 = (bf16[1,4,256,128]{3,2,1,0:T(8,128)(2,1)}, bf16[1,4,256,128]{3,2,1,0:T(8,128)(2,1)S(1)}, u32[]{:S(2)}, u32[]{:S(2)}) collective-permute-start(bf16[1,4,256,128]{3,2,1,0:T(8,128)(2,1)} %get-tuple-element.928), channel_id=1, source_target_pairs={{0,16},{2,18},{4,20},{6,22},{8,24},{10,26},{12,28},{14,30},{16,32}... | collective-permute-start | bytes 786440 | tf_op jit(solution)/shard_map/ppermute | solution.py:22
  68.9 18.3 %collective-permute-start.2 = (bf16[1,1,256,128]{3,2,1,0:T(8,128)(2,1)}, bf16[1,1,256,128]{3,2,1,0:T(8,128)(2,1)S(1)}, u32[]{:S(2)}, u32[]{:S(2)}) collective-permute-start(bf16[1,1,256,128]{3,2,1,0:T(8,128)(2,1)} %get-tuple-element.925), channel_id=1, source_target_pairs={{0,14},{2,16},{4,18},{6,20},{8,22},{10,24},{12,26},{14,28},{16,30}... | collective-permute-start | bytes 196616 | tf_op jit(solution)/shard_map/ppermute | solution.py:22
  74.2 16.1 %collective-permute-start.3 = (bf16[4,1,256,128]{3,2,1,0:T(8,128)(2,1)}, bf16[4,1,256,128]{3,2,1,0:T(8,128)(2,1)S(1)}, u32[]{:S(2)}, u32[]{:S(2)}) collective-permute-start(bf16[4,1,256,128]{3,2,1,0:T(8,128)(2,1)} %get-tuple-element.930), channel_id=1, source_target_pairs={{0,2},{2,4},{4,6},{6,8},{8,10},{10,12},{12,14},{14,16},{16,18},{18... | collective-permute-start | bytes 786440 | tf_op jit(solution)/shard_map/ppermute | solution.py:22
  79.6 10.8 collective-permute-start.4
  83.2 9.1 collective-permute-start.5
  84.5 14.3 %collective-permute-start.6 = (bf16[1,4,256,128]{3,2,1,0:T(8,128)(2,1)}, bf16[1,4,256,128]{3,2,1,0:T(8,128)(2,1)S(1)}, u32[]{:S(2)}, u32[]{:S(2)}) collective-permute-start(bf16[1,4,256,128]{3,2,1,0:T(8,128)(2,1)} %get-tuple-element.927), channel_id=1, source_target_pairs={{16,0},{18,2},{20,4},{22,6},{24,8},{26,10},{28,12},{30,14},{32,16}... | collective-permute-start | bytes 786440 | tf_op jit(solution)/shard_map/ppermute | solution.py:22
  87.2 11.7 collective-permute-start.7
  108.3 2.5 copy-start.4
  132.6 2.5 copy-start.4
  156.9 2.5 copy-start.4
  181.2 2.5 copy-start.4
  198.6 60.0 %all-reduce.6.cloned.1.call-start = ((), (), s32[]{:S(2)}) async-start(), calls=%async_computation.3 | async-start | bytes 2097152 | tf_op jit(solution)/shard_map/psum | solution.py:106
  231.9 408.5 %all-reduce.8.cloned.1.call-start = ((), (), s32[]{:S(2)}) async-start(), calls=%async_computation.4 | async-start | bytes 2097152 | tf_op jit(solution)/shard_map/psum | solution.py:106
  258.5 1.7 copy-start.2
  613.9 423.8 %all-gather.2.cloned.1.call-start = ((), (), s32[]{:S(2)}) async-start(), calls=%async_computation.5 | async-start | bytes 3145728 | tf_op jit(solution)/shard_map/all_gather | solution.py:176
  640.4 2.6 copy-start.3
  998.0 8.1 copy-start
  998.1 188.5 %reduce-scatter.5.cloned.1.call-start = ((), (), s32[]{:S(2)}) async-start(), calls=%async_computation.6 | async-start | bytes 7077888 | tf_op jit(solution)/shard_map/reduce_scatter | solution.py:212
  1000.5 21.3 %collective-permute-start.16 = (bf16[1,1,256,128]{3,2,1,0:T(8,128)(2,1)S(1)}, bf16[1,1,256,128]{3,2,1,0:T(8,128)(2,1)S(1)}, u32[]{:S(2)}, u32[]{:S(2)}) collective-permute-start(bf16[1,1,256,128]{3,2,1,0:T(8,128)(2,1)S(1)} %get-tuple-element.918), channel_id=1, source_target_pairs={{0,18},{2,20},{4,22},{6,24},{8,26},{10,28},{12,30},{14,32},{16,34}... | collective-permute-start | bytes 196616 | tf_op jit(solution)/shard_map/ppermute | solution.py:22
  1006.9 16.8 %collective-permute-start.17 = (bf16[1,4,256,128]{2,3,1,0:T(8,128)(2,1)S(1)}, bf16[1,4,256,128]{2,3,1,0:T(8,128)(2,1)S(1)}, u32[]{:S(2)}, u32[]{:S(2)}) collective-permute-start(bf16[1,4,256,128]{2,3,1,0:T(8,128)(2,1)S(1)} %get-tuple-element.920), channel_id=1, source_target_pairs={{0,16},{2,18},{4,20},{6,22},{8,24},{10,26},{12,28},{14,30},{16,32}... | collective-permute-start | bytes 786440 | tf_op jit(solution)/shard_map/ppermute | solution.py:22
  1010.0 17.2 %collective-permute-start.22 = (bf16[1,4,256,128]{2,3,1,0:T(8,128)(2,1)}, bf16[1,4,256,128]{2,3,1,0:T(8,128)(2,1)S(1)}, u32[]{:S(2)}, u32[]{:S(2)}) collective-permute-start(bf16[1,4,256,128]{2,3,1,0:T(8,128)(2,1)} %get-tuple-element.919), channel_id=1, source_target_pairs={{16,0},{18,2},{20,4},{22,6},{24,8},{26,10},{28,12},{30,14},{32,16}... | collective-permute-start | bytes 786440 | tf_op jit(solution)/shard_map/ppermute | solution.py:22
  1013.2 15.5 %collective-permute-start.18 = (bf16[1,1,256,128]{3,2,1,0:T(8,128)(2,1)}, bf16[1,1,256,128]{3,2,1,0:T(8,128)(2,1)S(1)}, u32[]{:S(2)}, u32[]{:S(2)}) collective-permute-start(bf16[1,1,256,128]{3,2,1,0:T(8,128)(2,1)} %get-tuple-element.917), channel_id=1, source_target_pairs={{0,14},{2,16},{4,18},{6,20},{8,22},{10,24},{12,26},{14,28},{16,30}... | collective-permute-start | bytes 196616 | tf_op jit(solution)/shard_map/ppermute | solution.py:22
  1016.9 15.0 %collective-permute-start.19 = (bf16[4,1,256,128]{3,2,1,0:T(8,128)(2,1)S(1)}, bf16[4,1,256,128]{3,2,1,0:T(8,128)(2,1)S(1)}, u32[]{:S(2)}, u32[]{:S(2)}) collective-permute-start(bf16[4,1,256,128]{3,2,1,0:T(8,128)(2,1)S(1)} %get-tuple-element.922), channel_id=1, source_target_pairs={{0,2},{2,4},{4,6},{6,8},{8,10},{10,12},{12,14},{14,16},{16,18},{18... | collective-permute-start | bytes 786440 | tf_op jit(solution)/shard_map/ppermute | solution.py:22
  1021.8 10.9 collective-permute-start.20
  1023.7 9.8 collective-permute-start.21
  1027.2 9.8 collective-permute-start.23
Sparse Core Ops, SparseCore 0:
  198.7 27.8 reduce-scatter.2
  232.0 26.4 all-reduce.5
  614.0 26.3 all-reduce.7
  998.2 14.1 all-gather.1
  1162.2 24.2 reduce-scatter.4
where the time goes:
time: 1210 us; the launch traced here: 1200 us
  other arithmetic  711 us (59%)
  matrix products  172 us (14%)
  waiting for transfers between devices  105 us (9%)
  starting transfers between devices  84 us (7%)
  local copies, waits for them, and re-layouts  62.3 us (5%)
  loops' own time  47.9 us (4%)
  between operations  14.5 us (1%)
    another operation x7, other arithmetic, apply_inverse(): lower_factor = jnp.linalg.cholesky(gram_sum)  377 us
    another operation x5, other arithmetic, apply_inverse(): lax.linalg.triangular_solve(lower_factor, identity, left_side=True, lower...  316 us
    dot_general x36, matrix products, couple_row(): jnp.einsum('brj,bjs->brs', projected, near_basis, preferred_element_type=...  85.2 us
    ppermute x24, starting transfers between devices, from_behind(): lax.ppermute(value, axis, [(source, source + steps) for source in range(i...  74.3 us
    dot_general x36, matrix products, sketch_row(): jnp.einsum('bij,bjr->ibr', block_vals, near_omega, preferred_element_type...  68.7 us
    psum x2, waiting for transfers between devices, orthonormal(): gram_sum = lax.psum(gram_sum, 'col')  43.5 us
    reduce_scatter x1, waiting for transfers between devices, body(): lax.psum_scatter(jnp.transpose(blocks, (1, 0, 2, 3)).reshape(half_points...  28 us
  transfers between devices with their start and end apart: 29, of which 7 were waited for; matrix products, arithmetic and copies ran while one was open for 4% of the time, Pallas kernels for 0%

commit v1 on v0

v1 whole, which is shorter than its diff:
```python
import functools
import math

import jax
import jax.numpy as jnp
import numpy as np
from jax import lax
from jax.experimental import pallas as pl
from jax.experimental.pallas import tpu as pltpu
from jax.sharding import PartitionSpec as P

MESH = pl.DeviceIdType.MESH
HIGHEST = lax.Precision.HIGHEST
TILE = 4
POINTS = 512
RANK = 128
FEATURES = 16
SLOTS = 9
LIMIT = 63 << 20
PANEL = 16
NT = (((1,), (1,)), ((), ()))
TN = (((0,), (0,)), ((), ()))
DIRECTIONS = [(dy, dx) for dy in (-1, 0, 1) for dx in (-1, 0, 1) if (dy, dx) != (0, 0)]


def slot_scales():
    unit = 2.0**13
    out = np.zeros((SLOTS, FEATURES, 1), np.float32)
    for slot in range(SLOTS):
        y, x = slot // 3 - 1, slot % 3 - 1
        out[slot, :, 0] = (
            [-2 * unit, -2 * unit, -unit / 8] + [unit] * 6
            + [-2 * unit * x, -2 * unit * y, 2 * unit * x, 2 * unit * y, unit * (x * x + y * y), 4.0, 0.0]
        )
    return out


def place(step, side, low, high):
    if step == -1:
        return low
    if step == 1:
        return high
    return slice(1, side + 1)


class Halo:
    def __init__(self, plate):
        self.plate = plate
        box, self.col = lax.axis_index("box"), lax.axis_index("col")
        self.row = box // plate * 2 + self.col
        self.column = box % plate
        self.partner = (box, 1 - self.col)

    def device(self, dy, dx):
        high = self.plate * 2
        row = (self.row + dy + high) % high
        column = (self.column + dx + self.plate) % self.plate
        return (row // 2 * self.plate + column, row % 2)

    def barrier(self):
        sem = pltpu.get_barrier_semaphore()
        for dy, dx in DIRECTIONS:
            pl.semaphore_signal(sem, inc=1, device_id=self.device(dy, dx), device_id_type=MESH)
        pl.semaphore_wait(sem, len(DIRECTIONS))

    def copies(self, ext, send, recv):
        made = []
        for n, (dy, dx) in enumerate(DIRECTIONS):
            made.append(
                pltpu.make_async_remote_copy(
                    src_ref=ext.at[place(dy, 2, 1, 2), place(dx, TILE, 1, TILE)],
                    dst_ref=ext.at[place(dy, 2, 3, 0), place(dx, TILE, TILE + 1, 0)],
                    send_sem=send.at[n],
                    recv_sem=recv.at[n],
                    device_id=self.device(dy, dx),
                    device_id_type=MESH,
                )
            )
        return made


def parts(value, count):
    made = []
    for _ in range(count):
        made.append(value.astype(jnp.bfloat16))
        value = value - made[-1].astype(jnp.float32)
    return made


def features(points_ref, row):
    wide = points_ref.astype(jnp.float32)
    u, v, h = wide[0:1], wide[1:2], wide[2:3]
    pieces = parts(u * u + v * v + h * h * 0.0625, 3)
    at = lax.broadcasted_iota(jnp.int32, (FEATURES, POINTS), 0)
    shifted, first = (9, 3) if row else (11, 6)
    out = jnp.where(at == FEATURES - 1, 0.0, 1.0)
    for place_of, value in ((0, u), (shifted, u), (1, v), (shifted + 1, v), (2, h)):
        out = jnp.where(at == place_of, value, out)
    for n in range(3):
        out = jnp.where(at == first + n, pieces[n].astype(jnp.float32), out)
    return out


def eliminate(a_ref, p_ref, panel_ref):
    boxes, rank = a_ref.shape[0], a_ref.shape[1]
    lane = lax.broadcasted_iota(jnp.int32, (boxes, rank), 1)
    row_id = lax.broadcasted_iota(jnp.int32, (rank, rank), 0)
    col_id = lax.broadcasted_iota(jnp.int32, (rank, rank), 1)

    def panel(n, carry):
        first = pl.multiple_of(n * PANEL, PANEL)
        for b in range(boxes):
            panel_ref[:, b, :] = a_ref[b, pl.ds(first, PANEL), :]
        rows = [panel_ref[i] for i in range(PANEL)]
        for k in range(PANEL):
            here = lane == first + k
            index = jnp.full((boxes, rank), first + k, jnp.int32)
            pivot = jnp.take_along_axis(rows[k], index, axis=1)
            inverse = 1.0 / pivot
            scaled = jnp.where(here, inverse, rows[k] * inverse)
            for i in range(k + 1, PANEL):
                factor = jnp.take_along_axis(rows[i], index, axis=1)
                rows[i] = jnp.where(here, 0.0, rows[i]) - factor * scaled
            keep = (lane < first + k) | (lane >= first + PANEL)
            rows[k] = jnp.where(keep, rows[k], jnp.where(here, 1.0, 0.0)) * lax.rsqrt(pivot)
        for i in range(PANEL):
            panel_ref[i] = rows[i]
        below = row_id >= first + PANEL
        inside = (col_id >= first) & (col_id < first + PANEL)
        for b in range(boxes):
            own = panel_ref[:, b, :]
            p_ref[b, pl.ds(first, PANEL), :] = jnp.where(col_id[:PANEL] <= row_id[:PANEL] + first, own, 0.0)
            w1, w2, w3 = parts(own, 3)
            left = jnp.concatenate([w1, w1, w2, w1, w2, w3], 0)
            right = jnp.concatenate([w1, w2, w1, w3, w2, w1], 0)
            update = lax.dot_general(left, right, TN, preferred_element_type=jnp.float32)
            old = a_ref[b]
            a_ref[b] = jnp.where(below, jnp.where(inside, 0.0, old) - update, old)
        return carry

    lax.fori_loop(0, rank // PANEL, panel, 0)


def kernel(
    plate, mask_ref, points_ref, sketch_ref, scale_ref, basis_ref, coupling_ref,
    ext_p, ext_e, ext_o, ext_b, kbuf, turned, y_ref, work, a_ref, p_ref, panel_ref, basis_t, stage,
    local_sem, out_sem, swap_send, swap_recv, p_send, p_recv, o_send, o_recv,
    b_send, b_recv, half_send, half_recv, c_send, c_recv,
):
    halo = Halo(plate)
    own, other = halo.col, 1 - halo.col
    half = sketch_ref.shape[1]
    rank_half = coupling_ref.shape[2]
    inner = slice(1, TILE + 1)
    mine = pl.ds(pl.multiple_of(own * half, half), half)
    theirs = pl.ds(pl.multiple_of(other * half, half), half)
    locals_p, locals_o, swaps = [], [], []
    for r in range(2):
        boxes = pl.ds(own * 8 + r * TILE, TILE)
        away = pl.ds(other * 8 + r * TILE, TILE)
        locals_p.append(pltpu.make_async_copy(points_ref.at[boxes], ext_p.at[1 + r, inner], local_sem.at[r]))
        locals_o.append(
            pltpu.make_async_copy(sketch_ref.at[boxes], ext_o.at[1 + r, inner, mine], local_sem.at[2 + r])
        )
        swaps.append(
            pltpu.make_async_remote_copy(
                src_ref=sketch_ref.at[away],
                dst_ref=ext_o.at[1 + r, inner, mine],
                send_sem=swap_send.at[r],
                recv_sem=swap_recv.at[r],
                device_id=halo.partner,
                device_id_type=MESH,
            )
        )
    for copy in locals_p + locals_o:
        copy.start()
    halo.barrier()
    for copy in swaps:
        copy.start()
    for copy in locals_p:
        copy.wait()
    p_copies = halo.copies(ext_p, p_send, p_recv)
    for copy in p_copies:
        copy.start()

    def own_features(b, carry):
        r, c = 1 + b // TILE, 1 + b % TILE
        value = ext_p[r, c]
        ext_e[r, c] = features(value, False)
        turned[b] = jnp.transpose(features(value, True)).astype(jnp.bfloat16)
        return carry

    lax.fori_loop(0, 8, own_features, 0)
    for copy in locals_o:
        copy.wait()
    for copy in swaps:
        copy.wait_recv()
    o_copies = halo.copies(ext_o, o_send, o_recv)
    for copy in o_copies:
        copy.start()

    def weight_of(b, slot):
        return mask_ref[own * 8 + b, slot].astype(jnp.float32)

    def first_term(b, carry):
        y_ref[b] = ext_o[1 + b // TILE, 1 + b % TILE].astype(jnp.float32) * weight_of(b, 4)
        return carry

    lax.fori_loop(0, 8, first_term, 0)

    def sketch_block(b, slot):
        r, c = b // TILE + slot // 3, b % TILE + slot % 3
        near = (ext_e[r, c] * scale_ref[slot]).astype(jnp.bfloat16)
        weight = weight_of(b, slot)
        step = 128
        for first in range(0, POINTS, step):
            rows = slice(first, first + step)
            square = jnp.dot(turned[b, rows, :], near, preferred_element_type=jnp.float32)
            values = lax.rsqrt(square).astype(jnp.bfloat16)
            kbuf[b, slot, rows, :] = values
            y_ref[b, rows, :] += jnp.dot(values, ext_o[r, c], preferred_element_type=jnp.float32) * weight

    def couple_block(b, slot):
        near = ext_b[b // TILE + slot // 3, b % TILE + slot % 3]
        moved = jnp.dot(kbuf[b, slot], near, preferred_element_type=jnp.float32).astype(jnp.bfloat16)
        value = jnp.dot(basis_t[b], moved, preferred_element_type=jnp.float32)
        stage[b, slot] = value * (weight_of(b, slot) * (1.0 / POINTS))
        keep, give = out_copies(pl.ds(b, 1), pl.ds(slot, 1), own * 8 + b, 1)
        keep.start()
        give.start()

    def out_copies(b, slot, first, count):
        kept = pl.ds(pl.multiple_of(own * rank_half, rank_half), rank_half)
        given = pl.ds(pl.multiple_of(other * rank_half, rank_half), rank_half)
        target = coupling_ref.at[pl.ds(first, count), slot]
        keep = pltpu.make_async_copy(stage.at[b, slot, kept], target, out_sem)
        give = pltpu.make_async_remote_copy(
            src_ref=stage.at[b, slot, given],
            dst_ref=target,
            send_sem=c_send,
            recv_sem=c_recv,
            device_id=halo.partner,
            device_id_type=MESH,
        )
        return keep, give

    def inner_blocks(block):
        def body(t, carry):
            r, q = t // 20, t % 20
            y, p = q // 10 * (1 - 2 * r), q % 10
            some, last = (p + 6) // 10, (p + 3) // 10
            x, c = some - 2 * last, p - 4 * some - 2 * last
            block(r * TILE + c, 3 * (y + 1) + x + 1)
            return carry

        lax.fori_loop(0, 40, body, 0)

    def outer_blocks(block):
        def across(t, carry):
            r, q = t // 12, t % 12
            block(r * TILE + q // 3, 6 * r + q % 3)
            return carry

        lax.fori_loop(0, 24, across, 0)

        def sides(t, carry):
            r, side, y = t // 4, t // 2 % 2, t % 2 * (1 - 2 * (t // 4))
            block(r * TILE + 3 * side, 3 * (y + 1) + 2 * side)
            return carry

        lax.fori_loop(0, 8, sides, 0)

    inner_blocks(sketch_block)
    for copy in p_copies:
        copy.wait_recv()

    def halo_features(t, carry):
        r, c = t // 6, t % 6
        ext_e[3 * r, c] = features(ext_p[3 * r, c], False)
        return carry

    lax.fori_loop(0, 12, halo_features, 0)

    def side_features(t, carry):
        r, c = 1 + t // 2, t % 2 * (TILE + 1)
        ext_e[r, c] = features(ext_p[r, c], False)
        return carry

    lax.fori_loop(0, 4, side_features, 0)
    for copy in o_copies:
        copy.wait_recv()
    outer_blocks(sketch_block)

    def add_units(b, carry):
        same = lax.broadcasted_iota(jnp.int32, (128, 128), 0) == lax.broadcasted_iota(jnp.int32, (128, 128), 1)
        unit = jnp.where(same, 1.0, 0.0)
        for first in range(0, POINTS, 128):
            part = slice(first, first + 128)
            kbuf[b, 4, part, part] = (kbuf[b, 4, part, part].astype(jnp.float32) + unit).astype(jnp.bfloat16)
        return carry

    lax.fori_loop(0, 8, add_units, 0)

    def first_gram(b, carry):
        value = y_ref[b]
        gram = lax.dot_general(value, value, TN, precision=HIGHEST, preferred_element_type=jnp.float32)
        a_ref[b] = gram * (1.0 / POINTS)
        return carry

    def first_apply(b, carry):
        work[b] = lax.dot_general(
            y_ref[b], p_ref[b], NT, precision=HIGHEST, preferred_element_type=jnp.float32
        )
        return carry

    def second_gram(b, carry):
        high, low = parts(work[b], 2)
        cross = lax.dot_general(high, low, TN, preferred_element_type=jnp.float32)
        gram = lax.dot_general(high, high, TN, preferred_element_type=jnp.float32) + (cross + cross.T)
        a_ref[b] = gram * (1.0 / POINTS)
        return carry

    def second_apply(b, carry):
        high, low = parts(work[b], 2)
        p_high, p_low = parts(p_ref[b], 2)
        value = lax.dot_general(high, p_high, NT, preferred_element_type=jnp.float32)
        value += lax.dot_general(high, p_low, NT, preferred_element_type=jnp.float32)
        value += lax.dot_general(low, p_high, NT, preferred_element_type=jnp.float32)
        ext_b[1 + b // TILE, 1 + b % TILE] = value.astype(jnp.bfloat16)
        return carry

    lax.fori_loop(0, 8, first_gram, 0)
    eliminate(a_ref, p_ref, panel_ref)
    lax.fori_loop(0, 8, first_apply, 0)
    lax.fori_loop(0, 8, second_gram, 0)
    eliminate(a_ref, p_ref, panel_ref)
    lax.fori_loop(0, 8, second_apply, 0)

    def turn_basis(b, carry):
        value = ext_b[1 + b // TILE, 1 + b % TILE].astype(jnp.float32)
        basis_t[b] = jnp.transpose(value).astype(jnp.bfloat16)
        return carry

    lax.fori_loop(0, 8, turn_basis, 0)
    b_copies = halo.copies(ext_b, b_send, b_recv)
    for copy in b_copies:
        copy.start()
    keeps, gives = [], []
    for r in range(2):
        boxes = pl.ds(own * 8 + r * TILE, TILE)
        keeps.append(
            pltpu.make_async_copy(ext_b.at[1 + r, inner, mine], basis_ref.at[boxes], local_sem.at[r])
        )
        gives.append(
            pltpu.make_async_remote_copy(
                src_ref=ext_b.at[1 + r, inner, theirs],
                dst_ref=basis_ref.at[boxes],
                send_sem=half_send.at[r],
                recv_sem=half_recv.at[r],
                device_id=halo.partner,
                device_id_type=MESH,
            )
        )
    for copy in keeps + gives:
        copy.start()
    inner_blocks(couple_block)
    for copy in b_copies:
        copy.wait_recv()
    outer_blocks(couple_block)
    keep, give = out_copies(slice(None), slice(None), own * 8, 8)
    keep.wait()
    give.wait()
    for copy in keeps + gives:
        copy.wait()
    for copy in swaps + p_copies + o_copies + b_copies:
        copy.wait_send()


def body(plate, points, sketch, near_mask, scale):
    boxes = points.shape[0]
    mine = boxes // 2
    vmem, hbm, smem = (pl.BlockSpec(memory_space=space) for space in (pltpu.VMEM, pl.ANY, pltpu.SMEM))
    dma = pltpu.SemaphoreType.DMA
    columns = pltpu.VMEM((4, TILE + 2, POINTS, RANK), jnp.bfloat16)
    tall = pltpu.VMEM((mine, POINTS, RANK), jnp.float32)
    square = pltpu.VMEM((mine, RANK, RANK), jnp.float32)
    return pl.pallas_call(
        functools.partial(kernel, plate),
        out_shape=(
            jax.ShapeDtypeStruct((boxes, POINTS // 2, RANK), jnp.bfloat16),
            jax.ShapeDtypeStruct((boxes, SLOTS, RANK // 2, RANK), jnp.float32),
        ),
        in_specs=[smem, hbm, hbm, vmem],
        out_specs=(hbm, hbm),
        scratch_shapes=[
            pltpu.VMEM((4, TILE + 2, 3, POINTS), jnp.bfloat16),
            pltpu.VMEM((4, TILE + 2, FEATURES, POINTS), jnp.float32),
            columns, columns,
            pltpu.VMEM((mine, SLOTS, POINTS, POINTS), jnp.bfloat16),
            pltpu.VMEM((mine, POINTS, FEATURES), jnp.bfloat16),
            tall, tall, square, square,
            pltpu.VMEM((PANEL, mine, RANK), jnp.float32),
            pltpu.VMEM((mine, RANK, POINTS), jnp.bfloat16),
            pltpu.VMEM((mine, SLOTS, RANK, RANK), jnp.float32),
            dma((4,)), dma, dma((2,)), dma((2,)), dma((8,)), dma((8,)), dma((8,)), dma((8,)),
            dma((8,)), dma((8,)), dma((2,)), dma((2,)), dma, dma,
        ],
        compiler_params=pltpu.CompilerParams(collective_id=0, has_side_effects=True, vmem_limit_bytes=LIMIT),
        name="plate_level",
    )(near_mask, points, sketch, scale)


def solution(mesh):
    plate = math.isqrt(mesh.shape["box"])

    def step(points, sketch, near_mask):
        return body(plate, points, sketch, near_mask, jnp.asarray(slot_scales()))

    return jax.shard_map(
        step,
        mesh=mesh,
        in_specs=(P("box", None, None), P("box", "col", None), P("box", None)),
        out_specs=(P("box", "col", None), P("box", None, "col", None)),
        check_vma=False,
    )
```

time: 1210 us -> 170 us (0.14)
  other arithmetic: 711 us -> 0 us
  matrix products: 172 us -> 0 us
  Pallas kernels: 0 us -> 160 us
  waiting for transfers between devices: 105 us -> 0 us
  starting transfers between devices: 84 us -> 0 us
  local copies, waits for them, and re-layouts: 62.3 us -> 9.01 us
  loops' own time: 47.9 us -> 0 us
  between operations: 14.5 us -> 0.64 us
    another operation x15 -> x0, other arithmetic: 696 us -> none  [the longest x7 377 us: apply_inverse(): lower_factor = jnp.linalg.cholesky(gram_sum)]
    dot_general x76 -> x0, matrix products: 169 us -> none  [the longest x36 85.2 us: couple_row(): jnp.einsum('brj,bjs->brs', projected, near_basis, preferred_element_type=...]
    pallas_call x0 -> x1, Pallas kernels: none -> 160 us  [body(): pl.pallas_call(functools.partial(kernel, plate), out_shape=(jax.ShapeDtyp...]
    ppermute x24 -> x0, starting transfers between devices: 74.3 us -> none  [from_behind(): lax.ppermute(value, axis, [(source, source + steps) for source in range(i...]
    reduce_scatter x2 -> x0, waiting for transfers between devices: 51.1 us -> none  [the longest x1 28 us: body(): lax.psum_scatter(jnp.transpose(blocks, (1, 0, 2, 3)).reshape(half_points...]
    another operation x2 -> x0, loops' own time: 47.9 us -> none  [the longest x1 24 us: body(): lax.map(couple_row, tile_rows).reshape(box_count, 9, skel_rank, skel_rank)]
    psum x2 -> x0, waiting for transfers between devices: 43.5 us -> none  [orthonormal(): gram_sum = lax.psum(gram_sum, 'col')]
    scatter x25 -> x0, local copies, waits for them, and re-layouts: 24.6 us -> none  [the longest x22 21.7 us: neighbours(): holder.at[landing(offset_y, tile_side), landing(offset_x, tile_side)]]
  transfers between devices with their start and end apart: 29 -> 0, of which waited for: 7 -> 0; matrix products, arithmetic and copies ran while one was open for 4% -> 0% of each run, Pallas kernels for 0% -> 0%
where the time goes in v1:
time: 170 us
  Pallas kernels  160 us (94%)
  local copies, waits for them, and re-layouts  9.01 us (5%)
    pallas_call x1, Pallas kernels, body(): pl.pallas_call(functools.partial(kernel, plate), out_shape=(jax.ShapeDtyp...  160 us
    unnamed x3, local copies, waits for them, and re-layouts  9.01 us

profile of v1, /device:TPU:1, one launch (start us, length us, event | category | flops | bytes accessed | tf_op | source)
XLA Modules:
  0.0 169.7 jit_solution(14141099143195075124)
XLA Ops:
  0.6 1.5 copy.6.points_ref
  2.1 160.0 %plate_level.1 = (bf16[16,256,128]{2,1,0:T(8,128)(2,1)}, f32[16,9,64,128]{3,2,1,0:T(8,128)}) custom-call(s32[16,9]{1,0:T(8,128)} %mask_ref.1, bf16[16,3,512]{2,1,0:T(4,128)(2,1)} %copy.6.points_ref, bf16[16,256,128]{2,1,0:T(8,128)(2,1)} %sketch_ref.1, f32[9,16,1]{2,1,0:T(8,128)} %constant.2.clone.scale_ref), custom_call_target="tpu_custom_call" | custom-call | tf_op jit(solution)/shard_map/plate_level/pallas_call | solution.py:387
  162.2 2.3 %copy.9 = bf16[16,256,128]{2,1,0:T(8,128)(2,1)} copy(bf16[16,256,128]{2,1,0:T(8,128)(2,1)} %get-tuple-element.4) | data formatting | bytes 2097152
  164.4 5.2 %copy.10 = f32[16,9,64,128]{3,2,1,0:T(8,128)} copy(f32[16,9,64,128]{3,2,1,0:T(8,128)} %get-tuple-element.5) | data formatting | bytes 9437184

commit v2 on v1

--- a/solution.py
+++ b/solution.py
@@ -3,7 +3,6 @@
 
 import jax
 import jax.numpy as jnp
-import numpy as np
 from jax import lax
 from jax.experimental import pallas as pl
 from jax.experimental.pallas import tpu as pltpu
@@ -14,25 +13,14 @@
 TILE = 4
 POINTS = 512
 RANK = 128
-FEATURES = 16
+FEATURES = 8
+SCALE = math.sqrt(8192.0)
 SLOTS = 9
 LIMIT = 63 << 20
 PANEL = 16
 NT = (((1,), (1,)), ((), ()))
 TN = (((0,), (0,)), ((), ()))
 DIRECTIONS = [(dy, dx) for dy in (-1, 0, 1) for dx in (-1, 0, 1) if (dy, dx) != (0, 0)]
-
-
-def slot_scales():
-    unit = 2.0**13
-    out = np.zeros((SLOTS, FEATURES, 1), np.float32)
-    for slot in range(SLOTS):
-        y, x = slot // 3 - 1, slot % 3 - 1
-        out[slot, :, 0] = (
-            [-2 * unit, -2 * unit, -unit / 8] + [unit] * 6
-            + [-2 * unit * x, -2 * unit * y, 2 * unit * x, 2 * unit * y, unit * (x * x + y * y), 4.0, 0.0]
-        )
-    return out
 
 
 def place(step, side, low, high):
@@ -87,18 +75,13 @@
     return made
 
 
-def features(points_ref, row):
-    wide = points_ref.astype(jnp.float32)
-    u, v, h = wide[0:1], wide[1:2], wide[2:3]
-    pieces = parts(u * u + v * v + h * h * 0.0625, 3)
+def features(points):
+    wide = points.astype(jnp.float32)
+    u, v = (wide[0:1] - 0.5) * SCALE, (wide[1:2] - 0.5) * SCALE
+    h = (wide[2:3] - 0.5) * (0.25 * SCALE)
     at = lax.broadcasted_iota(jnp.int32, (FEATURES, POINTS), 0)
-    shifted, first = (9, 3) if row else (11, 6)
-    out = jnp.where(at == FEATURES - 1, 0.0, 1.0)
-    for place_of, value in ((0, u), (shifted, u), (1, v), (shifted + 1, v), (2, h)):
-        out = jnp.where(at == place_of, value, out)
-    for n in range(3):
-        out = jnp.where(at == first + n, pieces[n].astype(jnp.float32), out)
-    return out
+    rest = jnp.where(at == 2, h, u * u + v * v + h * h)
+    return jnp.where(at == 0, u, jnp.where(at == 1, v, rest))
 
 
 def eliminate(a_ref, p_ref, panel_ref):
@@ -141,9 +124,35 @@
     lax.fori_loop(0, rank // PANEL, panel, 0)
 
 
+def block_of(t):
+    rest, side = t // 40, t // 64
+    r, q = t // 20, t % 20
+    y, p = q // 10 * (1 - 2 * r), q % 10
+    some, last = (p + 6) // 10, (p + 3) // 10
+    inner_b = r * TILE + p - 4 * some - 2 * last
+    inner_slot = 3 * (y + 1) + some - 2 * last + 1
+    n = t - 40
+    r, q = n // 12, n % 12
+    across_b, across_slot = r * TILE + q // 3, 6 * r + q % 3
+    n = t - 64
+    r, right, y = n // 4, n // 2 % 2, n % 2 * (1 - 2 * (n // 4))
+    side_b, side_slot = r * TILE + 3 * right, 3 * (y + 1) + 2 * right
+    b = inner_b * (1 - rest) + across_b * (rest - side) + side_b * side
+    slot = inner_slot * (1 - rest) + across_slot * (rest - side) + side_slot * side
+    return b, slot
+
+
+def pair_of(u):
+    below, down, back = (u + 10) // 16, (u + 6) // 16, (u + 3) // 16
+    r = u // 3 * (1 - below)
+    c = u % 3 * (1 - below) + (u - 6) * (below - down) + (u - 10) * (down - back) + (u - 12) * back
+    x = 1 - below + down - 2 * back
+    return r * TILE + c, 3 * (below + 1) + x + 1
+
+
 def kernel(
-    plate, mask_ref, points_ref, sketch_ref, scale_ref, basis_ref, coupling_ref,
-    ext_p, ext_e, ext_o, ext_b, kbuf, turned, y_ref, work, a_ref, p_ref, panel_ref, basis_t, stage,
+    plate, mask_ref, points_ref, sketch_ref, basis_ref, coupling_ref,
+    ext_p, ext_e, ext_o, ext_b, kbuf, even, odd, turned, y_ref, work, a_ref, p_ref, panel_ref, basis_t, stage,
     local_sem, out_sem, swap_send, swap_recv, p_send, p_recv, o_send, o_recv,
     b_send, b_recv, half_send, half_recv, c_send, c_recv,
 ):
@@ -185,9 +194,9 @@
 
     def own_features(b, carry):
         r, c = 1 + b // TILE, 1 + b % TILE
-        value = ext_p[r, c]
-        ext_e[r, c] = features(value, False)
-        turned[b] = jnp.transpose(features(value, True)).astype(jnp.bfloat16)
+        value = features(ext_p[r, c])
+        ext_e[r, c] = value
+        turned[b] = jnp.transpose(value)
         return carry
 
     lax.fori_loop(0, 8, own_features, 0)
@@ -208,23 +217,54 @@
 
     lax.fori_loop(0, 8, first_term, 0)
 
-    def sketch_block(b, slot):
-        r, c = b // TILE + slot // 3, b % TILE + slot % 3
-        near = (ext_e[r, c] * scale_ref[slot]).astype(jnp.bfloat16)
-        weight = weight_of(b, slot)
-        step = 128
+    def fill_block(t, copy_ref):
+        b, slot = block_of(t)
+        near = ext_e[b // TILE + slot // 3, b % TILE + slot % 3]
+        u = near[0:1] + (slot % 3 - 1) * SCALE
+        v = near[1:2] + (slot // 3 - 1) * SCALE
+        h = near[2:3]
+        norm = u * u + v * v + h * h + 4.0
+        u, v, h = -2.0 * u, -2.0 * v, -2.0 * h
+        step = 64
         for first in range(0, POINTS, step):
             rows = slice(first, first + step)
-            square = jnp.dot(turned[b, rows, :], near, preferred_element_type=jnp.float32)
+            own_rows = turned[b, rows, :]
+            square = (own_rows[:, 3:4] + norm) + own_rows[:, 0:1] * u
+            square = square + (own_rows[:, 1:2] * v + own_rows[:, 2:3] * h)
             values = lax.rsqrt(square).astype(jnp.bfloat16)
             kbuf[b, slot, rows, :] = values
-            y_ref[b, rows, :] += jnp.dot(values, ext_o[r, c], preferred_element_type=jnp.float32) * weight
-
-    def couple_block(b, slot):
-        near = ext_b[b // TILE + slot // 3, b % TILE + slot % 3]
-        moved = jnp.dot(kbuf[b, slot], near, preferred_element_type=jnp.float32).astype(jnp.bfloat16)
-        value = jnp.dot(basis_t[b], moved, preferred_element_type=jnp.float32)
-        stage[b, slot] = value * (weight_of(b, slot) * (1.0 / POINTS))
+            copy_ref[rows, :] = values
+
+    def add_block(t, copy_ref):
+        b, slot = block_of(t)
+        near = ext_o[b // TILE + slot // 3, b % TILE + slot % 3]
+        y_ref[b] += jnp.dot(copy_ref[...], near, preferred_element_type=jnp.float32) * weight_of(b, slot)
+
+    def sketch_pair(i, carry):
+        t = 2 * i
+        add_block(t, even)
+        fill_block(t + 1, odd)
+        add_block(t + 1, odd)
+        fill_block(jnp.minimum(t + 2, 71), even)
+        return carry
+
+    def couple_blocks(blocks, mirrored):
+        moved = []
+        for b, slot in blocks:
+            value = jnp.dot(basis_t[b], kbuf[b, slot], preferred_element_type=jnp.float32)
+            moved.append(value.astype(jnp.bfloat16))
+        for (b, slot), value in zip(blocks, moved):
+            y, x = slot // 3 - 1, slot % 3 - 1
+            near = ext_b[b // TILE + 1 + y, b % TILE + 1 + x]
+            value = jnp.dot(value, near, preferred_element_type=jnp.float32) * (1.0 / POINTS)
+            stage[b, slot] = value * weight_of(b, slot)
+            start_out(b, slot)
+            if mirrored:
+                other_b = b + TILE * y + x
+                stage[other_b, 8 - slot] = value.T * weight_of(other_b, 8 - slot)
+                start_out(other_b, 8 - slot)
+
+    def start_out(b, slot):
         keep, give = out_copies(pl.ds(b, 1), pl.ds(slot, 1), own * 8 + b, 1)
         keep.start()
         give.start()
@@ -244,52 +284,27 @@
         )
         return keep, give
 
-    def inner_blocks(block):
-        def body(t, carry):
-            r, q = t // 20, t % 20
-            y, p = q // 10 * (1 - 2 * r), q % 10
-            some, last = (p + 6) // 10, (p + 3) // 10
-            x, c = some - 2 * last, p - 4 * some - 2 * last
-            block(r * TILE + c, 3 * (y + 1) + x + 1)
-            return carry
-
-        lax.fori_loop(0, 40, body, 0)
-
-    def outer_blocks(block):
-        def across(t, carry):
-            r, q = t // 12, t % 12
-            block(r * TILE + q // 3, 6 * r + q % 3)
-            return carry
-
-        lax.fori_loop(0, 24, across, 0)
-
-        def sides(t, carry):
-            r, side, y = t // 4, t // 2 % 2, t % 2 * (1 - 2 * (t // 4))
-            block(r * TILE + 3 * side, 3 * (y + 1) + 2 * side)
-            return carry
-
-        lax.fori_loop(0, 8, sides, 0)
-
-    inner_blocks(sketch_block)
+    fill_block(0, even)
+    lax.fori_loop(0, 19, sketch_pair, 0)
     for copy in p_copies:
         copy.wait_recv()
 
     def halo_features(t, carry):
         r, c = t // 6, t % 6
-        ext_e[3 * r, c] = features(ext_p[3 * r, c], False)
+        ext_e[3 * r, c] = features(ext_p[3 * r, c])
         return carry
 
     lax.fori_loop(0, 12, halo_features, 0)
 
     def side_features(t, carry):
         r, c = 1 + t // 2, t % 2 * (TILE + 1)
-        ext_e[r, c] = features(ext_p[r, c], False)
+        ext_e[r, c] = features(ext_p[r, c])
         return carry
 
     lax.fori_loop(0, 4, side_features, 0)
     for copy in o_copies:
         copy.wait_recv()
-    outer_blocks(sketch_block)
+    lax.fori_loop(19, 36, sketch_pair, 0)
 
     def add_units(b, carry):
         same = lax.broadcasted_iota(jnp.int32, (128, 128), 0) == lax.broadcasted_iota(jnp.int32, (128, 128), 1)
@@ -363,10 +378,24 @@
         )
     for copy in keeps + gives:
         copy.start()
-    inner_blocks(couple_block)
+
+    def couple_centres(i, carry):
+        couple_blocks([(2 * i, 4), (2 * i + 1, 4)], False)
+        return carry
+
+    def couple_pairs(i, carry):
+        couple_blocks([pair_of(2 * i), pair_of(2 * i + 1)], True)
+        return carry
+
+    def couple_rest(i, carry):
+        couple_blocks([block_of(2 * i), block_of(2 * i + 1)], False)
+        return carry
+
+    lax.fori_loop(0, 4, couple_centres, 0)
+    lax.fori_loop(0, 8, couple_pairs, 0)
     for copy in b_copies:
         copy.wait_recv()
-    outer_blocks(couple_block)
+    lax.fori_loop(20, 36, couple_rest, 0)
     keep, give = out_copies(slice(None), slice(None), own * 8, 8)
     keep.wait()
     give.wait()
@@ -376,10 +405,10 @@
         copy.wait_send()
 
 
-def body(plate, points, sketch, near_mask, scale):
+def body(plate, points, sketch, near_mask):
     boxes = points.shape[0]
     mine = boxes // 2
-    vmem, hbm, smem = (pl.BlockSpec(memory_space=space) for space in (pltpu.VMEM, pl.ANY, pltpu.SMEM))
+    hbm, smem = (pl.BlockSpec(memory_space=space) for space in (pl.ANY, pltpu.SMEM))
     dma = pltpu.SemaphoreType.DMA
     columns = pltpu.VMEM((4, TILE + 2, POINTS, RANK), jnp.bfloat16)
     tall = pltpu.VMEM((mine, POINTS, RANK), jnp.float32)
@@ -390,14 +419,16 @@
             jax.ShapeDtypeStruct((boxes, POINTS // 2, RANK), jnp.bfloat16),
             jax.ShapeDtypeStruct((boxes, SLOTS, RANK // 2, RANK), jnp.float32),
         ),
-        in_specs=[smem, hbm, hbm, vmem],
+        in_specs=[smem, hbm, hbm],
         out_specs=(hbm, hbm),
         scratch_shapes=[
             pltpu.VMEM((4, TILE + 2, 3, POINTS), jnp.bfloat16),
             pltpu.VMEM((4, TILE + 2, FEATURES, POINTS), jnp.float32),
             columns, columns,
             pltpu.VMEM((mine, SLOTS, POINTS, POINTS), jnp.bfloat16),
-            pltpu.VMEM((mine, POINTS, FEATURES), jnp.bfloat16),
+            pltpu.VMEM((POINTS, POINTS), jnp.bfloat16),
+            pltpu.VMEM((POINTS, POINTS), jnp.bfloat16),
+            pltpu.VMEM((mine, POINTS, FEATURES), jnp.float32),
             tall, tall, square, square,
             pltpu.VMEM((PANEL, mine, RANK), jnp.float32),
             pltpu.VMEM((mine, RANK, POINTS), jnp.bfloat16),
@@ -407,14 +438,14 @@
         ],
         compiler_params=pltpu.CompilerParams(collective_id=0, has_side_effects=True, vmem_limit_bytes=LIMIT),
         name="plate_level",
-    )(near_mask, points, sketch, scale)
+    )(near_mask, points, sketch)
 
 
 def solution(mesh):
     plate = math.isqrt(mesh.shape["box"])
 
     def step(points, sketch, near_mask):
-        return body(plate, points, sketch, near_mask, jnp.asarray(slot_scales()))
+        return body(plate, points, sketch, near_mask)
 
     return jax.shard_map(
         step,

time: 170 us -> 138 us (0.81)
  Pallas kernels: 160 us -> 128 us
    pallas_call x1, Pallas kernels: 160 us -> 128 us  [body(): pl.pallas_call(functools.partial(kernel, plate), out_shape=(jax.ShapeDtyp...]
where the time goes in v2:
time: 138 us
  Pallas kernels  128 us (93%)
  local copies, waits for them, and re-layouts  9.01 us (7%)
    pallas_call x1, Pallas kernels, body(): pl.pallas_call(functools.partial(kernel, plate), out_shape=(jax.ShapeDtyp...  128 us
    unnamed x3, local copies, waits for them, and re-layouts  9.01 us

profile of v2, /device:TPU:1, one launch (start us, length us, event | category | flops | bytes accessed | tf_op | source)
XLA Modules:
  0.0 137.9 jit_solution(3968367329263671517)
XLA Ops:
  0.6 1.5 %copy.5.points_ref = bf16[16,3,512]{2,1,0:T(4,128)(2,1)} copy(bf16[16,3,512]{2,0,1:T(8,128)(2,1)} %param.3) | data formatting | bytes 98304 | tf_op args[0]
  2.1 128.2 %plate_level.1 = (bf16[16,256,128]{2,1,0:T(8,128)(2,1)}, f32[16,9,64,128]{3,2,1,0:T(8,128)}) custom-call(s32[16,9]{1,0:T(8,128)} %mask_ref.1, bf16[16,3,512]{2,1,0:T(4,128)(2,1)} %copy.5.points_ref, bf16[16,256,128]{2,1,0:T(8,128)(2,1)} %sketch_ref.1), custom_call_target="tpu_custom_call" | custom-call | tf_op jit(solution)/shard_map/plate_level/pallas_call | solution.py:416
  130.4 2.3 %copy.8 = bf16[16,256,128]{2,1,0:T(8,128)(2,1)} copy(bf16[16,256,128]{2,1,0:T(8,128)(2,1)} %get-tuple-element.4) | data formatting | bytes 2097152
  132.7 5.2 %copy.9 = f32[16,9,64,128]{3,2,1,0:T(8,128)} copy(f32[16,9,64,128]{3,2,1,0:T(8,128)} %get-tuple-element.5) | data formatting | bytes 9437184

commit v3 on v2

--- a/solution.py
+++ b/solution.py
@@ -51,12 +51,14 @@
             pl.semaphore_signal(sem, inc=1, device_id=self.device(dy, dx), device_id_type=MESH)
         pl.semaphore_wait(sem, len(DIRECTIONS))
 
-    def copies(self, ext, send, recv):
+    def copies(self, own, at, ext, send, recv):
         made = []
         for n, (dy, dx) in enumerate(DIRECTIONS):
+            rows = (slice(at, at + 2), at, at + 1)
+            columns = (slice(at, at + TILE), at, at + TILE - 1)
             made.append(
                 pltpu.make_async_remote_copy(
-                    src_ref=ext.at[place(dy, 2, 1, 2), place(dx, TILE, 1, TILE)],
+                    src_ref=own.at[rows[0 if dy == 0 else (3 + dy) // 2], columns[0 if dx == 0 else (3 + dx) // 2]],
                     dst_ref=ext.at[place(dy, 2, 3, 0), place(dx, TILE, TILE + 1, 0)],
                     send_sem=send.at[n],
                     recv_sem=recv.at[n],
@@ -95,17 +97,28 @@
         for b in range(boxes):
             panel_ref[:, b, :] = a_ref[b, pl.ds(first, PANEL), :]
         rows = [panel_ref[i] for i in range(PANEL)]
-        for k in range(PANEL):
-            here = lane == first + k
+        for k in range(0, PANEL, 2):
+            here, there = lane == first + k, lane == first + k + 1
+            both = here | there
             index = jnp.full((boxes, rank), first + k, jnp.int32)
-            pivot = jnp.take_along_axis(rows[k], index, axis=1)
-            inverse = 1.0 / pivot
-            scaled = jnp.where(here, inverse, rows[k] * inverse)
-            for i in range(k + 1, PANEL):
-                factor = jnp.take_along_axis(rows[i], index, axis=1)
-                rows[i] = jnp.where(here, 0.0, rows[i]) - factor * scaled
-            keep = (lane < first + k) | (lane >= first + PANEL)
-            rows[k] = jnp.where(keep, rows[k], jnp.where(here, 1.0, 0.0)) * lax.rsqrt(pivot)
+            upper, lower = rows[k], rows[k + 1]
+            p = jnp.take_along_axis(upper, index, axis=1)
+            q = jnp.take_along_axis(lower, index, axis=1)
+            s = jnp.take_along_axis(lower, index + 1, axis=1)
+            det = p * s - q * q
+            ratio = 1.0 / p
+            last = (1.0 / det) * p
+            share = q * ratio
+            upper = jnp.where(both, jnp.where(here, 1.0, 0.0), upper)
+            lower = jnp.where(both, jnp.where(there, 1.0, 0.0), lower) - share * upper
+            x, y = upper * ratio, lower * last
+            for i in range(k + 2, PANEL):
+                f = jnp.take_along_axis(rows[i], index, axis=1)
+                g = jnp.take_along_axis(rows[i], index + 1, axis=1) - f * share
+                rows[i] = (jnp.where(both, 0.0, rows[i]) - f * x) - g * y
+            outside = (lane < first) | (lane >= first + PANEL)
+            rows[k] = jnp.where(outside | (lane <= first + k), upper, 0.0) * lax.rsqrt(p)
+            rows[k + 1] = jnp.where(outside | (lane <= first + k + 1), lower, 0.0) * lax.sqrt(last)
         for i in range(PANEL):
             panel_ref[i] = rows[i]
         below = row_id >= first + PANEL
@@ -152,9 +165,9 @@
 
 def kernel(
     plate, mask_ref, points_ref, sketch_ref, basis_ref, coupling_ref,
-    ext_p, ext_e, ext_o, ext_b, kbuf, even, odd, turned, y_ref, work, a_ref, p_ref, panel_ref, basis_t, stage,
+    ext_p, ext_e, ext_o, ext_b, ext_d, rough, kbuf, even, odd, turned, y_ref, work, a_ref, p_ref, panel_ref, scale_ref, basis_t, stage,
     local_sem, out_sem, swap_send, swap_recv, p_send, p_recv, o_send, o_recv,
-    b_send, b_recv, half_send, half_recv, c_send, c_recv,
+    b_send, b_recv, d_send, d_recv, half_send, half_recv, c_send, c_recv,
 ):
     halo = Halo(plate)
     own, other = halo.col, 1 - halo.col
@@ -188,7 +201,7 @@
         copy.start()
     for copy in locals_p:
         copy.wait()
-    p_copies = halo.copies(ext_p, p_send, p_recv)
+    p_copies = halo.copies(ext_p, 1, ext_p, p_send, p_recv)
     for copy in p_copies:
         copy.start()
 
@@ -204,7 +217,7 @@
         copy.wait()
     for copy in swaps:
         copy.wait_recv()
-    o_copies = halo.copies(ext_o, o_send, o_recv)
+    o_copies = halo.copies(ext_o, 1, ext_o, o_send, o_recv)
     for copy in o_copies:
         copy.start()
 
@@ -319,13 +332,19 @@
     def first_gram(b, carry):
         value = y_ref[b]
         gram = lax.dot_general(value, value, TN, precision=HIGHEST, preferred_element_type=jnp.float32)
-        a_ref[b] = gram * (1.0 / POINTS)
+        at = [lax.broadcasted_iota(jnp.int32, (RANK, RANK), axis) for axis in (0, 1)]
+        diagonal = jnp.where(at[0] == at[1], gram, 0.0)
+        along, across = [lax.rsqrt(jnp.sum(diagonal, axis=axis, keepdims=True)) for axis in (0, 1)]
+        a_ref[b] = gram * along * across
+        scale_ref[b] = jnp.broadcast_to(along * math.sqrt(POINTS), (8, RANK))
         return carry
 
     def first_apply(b, carry):
-        work[b] = lax.dot_general(
-            y_ref[b], p_ref[b], NT, precision=HIGHEST, preferred_element_type=jnp.float32
+        value = lax.dot_general(
+            y_ref[b], p_ref[b] * scale_ref[b, 0:1], NT, precision=HIGHEST, preferred_element_type=jnp.float32
         )
+        work[b] = value
+        rough[b // TILE, b % TILE] = value.astype(jnp.bfloat16)
         return carry
 
     def second_gram(b, carry):
@@ -348,8 +367,22 @@
     eliminate(a_ref, p_ref, panel_ref)
     lax.fori_loop(0, 8, first_apply, 0)
     lax.fori_loop(0, 8, second_gram, 0)
+    b_copies = halo.copies(rough, 0, ext_b, b_send, b_recv)
+    for copy in b_copies:
+        copy.start()
     eliminate(a_ref, p_ref, panel_ref)
+
+    def step_of(b, carry):
+        at = [lax.broadcasted_iota(jnp.int32, (RANK, RANK), axis) for axis in (0, 1)]
+        step = p_ref[b] - jnp.where(at[0] == at[1], 1.0, 0.0)
+        ext_d[1 + b // TILE, 1 + b % TILE] = step.astype(jnp.bfloat16)
+        return carry
+
+    lax.fori_loop(0, 8, step_of, 0)
     lax.fori_loop(0, 8, second_apply, 0)
+    d_copies = halo.copies(ext_d, 1, ext_d, d_send, d_recv)
+    for copy in d_copies:
+        copy.start()
 
     def turn_basis(b, carry):
         value = ext_b[1 + b // TILE, 1 + b % TILE].astype(jnp.float32)
@@ -357,9 +390,6 @@
         return carry
 
     lax.fori_loop(0, 8, turn_basis, 0)
-    b_copies = halo.copies(ext_b, b_send, b_recv)
-    for copy in b_copies:
-        copy.start()
     keeps, gives = [], []
     for r in range(2):
         boxes = pl.ds(own * 8 + r * TILE, TILE)
@@ -393,15 +423,31 @@
 
     lax.fori_loop(0, 4, couple_centres, 0)
     lax.fori_loop(0, 8, couple_pairs, 0)
-    for copy in b_copies:
+    for copy in b_copies + d_copies:
         copy.wait_recv()
+
+    def finish_near(r, c):
+        near = ext_b[r, c]
+        change = lax.dot_general(near, ext_d[r, c], NT, preferred_element_type=jnp.float32)
+        ext_b[r, c] = (near.astype(jnp.float32) + change).astype(jnp.bfloat16)
+
+    def finish_across(t, carry):
+        finish_near(3 * (t // 6), t % 6)
+        return carry
+
+    def finish_side(t, carry):
+        finish_near(1 + t // 2, t % 2 * (TILE + 1))
+        return carry
+
+    lax.fori_loop(0, 12, finish_across, 0)
+    lax.fori_loop(0, 4, finish_side, 0)
     lax.fori_loop(20, 36, couple_rest, 0)
     keep, give = out_copies(slice(None), slice(None), own * 8, 8)
     keep.wait()
     give.wait()
     for copy in keeps + gives:
         copy.wait()
-    for copy in swaps + p_copies + o_copies + b_copies:
+    for copy in swaps + p_copies + o_copies + b_copies + d_copies:
         copy.wait_send()
 
 
@@ -425,16 +471,19 @@
             pltpu.VMEM((4, TILE + 2, 3, POINTS), jnp.bfloat16),
             pltpu.VMEM((4, TILE + 2, FEATURES, POINTS), jnp.float32),
             columns, columns,
+            pltpu.VMEM((4, TILE + 2, RANK, RANK), jnp.bfloat16),
+            pltpu.VMEM((2, TILE, POINTS, RANK), jnp.bfloat16),
             pltpu.VMEM((mine, SLOTS, POINTS, POINTS), jnp.bfloat16),
             pltpu.VMEM((POINTS, POINTS), jnp.bfloat16),
             pltpu.VMEM((POINTS, POINTS), jnp.bfloat16),
             pltpu.VMEM((mine, POINTS, FEATURES), jnp.float32),
             tall, tall, square, square,
             pltpu.VMEM((PANEL, mine, RANK), jnp.float32),
+            pltpu.VMEM((mine, 8, RANK), jnp.float32),
             pltpu.VMEM((mine, RANK, POINTS), jnp.bfloat16),
             pltpu.VMEM((mine, SLOTS, RANK, RANK), jnp.float32),
             dma((4,)), dma, dma((2,)), dma((2,)), dma((8,)), dma((8,)), dma((8,)), dma((8,)),
-            dma((8,)), dma((8,)), dma((2,)), dma((2,)), dma, dma,
+            dma((8,)), dma((8,)), dma((8,)), dma((8,)), dma((2,)), dma((2,)), dma, dma,
         ],
         compiler_params=pltpu.CompilerParams(collective_id=0, has_side_effects=True, vmem_limit_bytes=LIMIT),
         name="plate_level",

time: 138 us -> 127 us (0.920)
  Pallas kernels: 128 us -> 117 us
    pallas_call x1, Pallas kernels: 128 us -> 117 us  [body(): pl.pallas_call(functools.partial(kernel, plate), out_shape=(jax.ShapeDtyp...]
where the time goes in v3:
time: 127 us; the launch traced here: 126 us
  Pallas kernels  117 us (92%)
  local copies, waits for them, and re-layouts  9.01 us (7%)
    pallas_call x1, Pallas kernels, body(): pl.pallas_call(functools.partial(kernel, plate), out_shape=(jax.ShapeDtyp...  117 us
    unnamed x3, local copies, waits for them, and re-layouts  9.01 us

profile of v3, /device:TPU:1, one launch (start us, length us, event | category | flops | bytes accessed | tf_op | source)
XLA Modules:
  0.0 126.2 jit_solution(8749366987101909265)
XLA Ops:
  0.6 1.5 %copy.5.points_ref = bf16[16,3,512]{2,1,0:T(4,128)(2,1)} copy(bf16[16,3,512]{2,0,1:T(8,128)(2,1)} %param.3) | data formatting | bytes 98304 | tf_op args[0]
  2.1 116.6 %plate_level.1 = (bf16[16,256,128]{2,1,0:T(8,128)(2,1)}, f32[16,9,64,128]{3,2,1,0:T(8,128)}) custom-call(s32[16,9]{1,0:T(8,128)} %mask_ref.1, bf16[16,3,512]{2,1,0:T(4,128)(2,1)} %copy.5.points_ref, bf16[16,256,128]{2,1,0:T(8,128)(2,1)} %sketch_ref.1), custom_call_target="tpu_custom_call" | custom-call | tf_op jit(solution)/shard_map/plate_level/pallas_call | solution.py:462
  118.7 2.3 %copy.8 = bf16[16,256,128]{2,1,0:T(8,128)(2,1)} copy(bf16[16,256,128]{2,1,0:T(8,128)(2,1)} %get-tuple-element.4) | data formatting | bytes 2097152
  121.0 5.2 %copy.9 = f32[16,9,64,128]{3,2,1,0:T(8,128)} copy(f32[16,9,64,128]{3,2,1,0:T(8,128)} %get-tuple-element.5) | data formatting | bytes 9437184

commit v4 on v3

--- a/solution.py
+++ b/solution.py
@@ -67,6 +67,20 @@
                 )
             )
         return made
+
+
+def await_row(halo, near_core, ext, send, recv):
+    side = halo.col if near_core else 1 - halo.col
+    for n, columns in enumerate((TILE + 1, slice(1, TILE + 1), 0)):
+        landed = ext.at[3 * (1 - side), columns]
+        pltpu.make_async_remote_copy(
+            src_ref=landed,
+            dst_ref=landed,
+            send_sem=send.at[5 * side + n],
+            recv_sem=recv.at[5 * side + n],
+            device_id=halo.partner,
+            device_id_type=MESH,
+        ).wait_recv()
 
 
 def parts(value, count):
@@ -137,22 +151,24 @@
     lax.fori_loop(0, rank // PANEL, panel, 0)
 
 
-def block_of(t):
-    rest, side = t // 40, t // 64
-    r, q = t // 20, t % 20
-    y, p = q // 10 * (1 - 2 * r), q % 10
+def block_of(t, own):
+    marks = [t // 40, (t + 22) // 72, (t + 20) // 72, (t + 12) // 72]
+    p = t % 10
     some, last = (p + 6) // 10, (p + 3) // 10
-    inner_b = r * TILE + p - 4 * some - 2 * last
-    inner_slot = 3 * (y + 1) + some - 2 * last + 1
-    n = t - 40
-    r, q = n // 12, n % 12
-    across_b, across_slot = r * TILE + q // 3, 6 * r + q % 3
-    n = t - 64
-    r, right, y = n // 4, n // 2 % 2, n % 2 * (1 - 2 * (n // 4))
-    side_b, side_slot = r * TILE + 3 * right, 3 * (y + 1) + 2 * right
-    b = inner_b * (1 - rest) + across_b * (rest - side) + side_b * side
-    slot = inner_slot * (1 - rest) + across_slot * (rest - side) + side_slot * side
-    return b, slot
+    c, x = p - 4 * some - 2 * last, some - 2 * last
+    r = t // 20
+    steps = [(r, c, t % 20 // 10 * (1 - 2 * r), x), (1 - own, c, 1 - 2 * own, x)]
+    n = t - 50
+    steps.append((1 - own, 3 * n, 1 - 2 * own, 2 * n - 1))
+    n = t - 52
+    r, right = n // 4, n // 2 % 2
+    steps.append((r, 3 * right, n % 2 * (1 - 2 * r), 2 * right - 1))
+    n = t - 60
+    steps.append((own, n // 3, 2 * own - 1, n % 3 - 1))
+    r, c, y, x = steps[0]
+    for mark, before, after in zip(marks, steps, steps[1:]):
+        r, c, y, x = [now + mark * (b - a) for now, a, b in zip((r, c, y, x), before, after)]
+    return r * TILE + c, 3 * (y + 1) + x + 1
 
 
 def pair_of(u):
@@ -231,7 +247,7 @@
     lax.fori_loop(0, 8, first_term, 0)
 
     def fill_block(t, copy_ref):
-        b, slot = block_of(t)
+        b, slot = block_of(t, own)
         near = ext_e[b // TILE + slot // 3, b % TILE + slot % 3]
         u = near[0:1] + (slot % 3 - 1) * SCALE
         v = near[1:2] + (slot // 3 - 1) * SCALE
@@ -249,7 +265,7 @@
             copy_ref[rows, :] = values
 
     def add_block(t, copy_ref):
-        b, slot = block_of(t)
+        b, slot = block_of(t, own)
         near = ext_o[b // TILE + slot // 3, b % TILE + slot % 3]
         y_ref[b] += jnp.dot(copy_ref[...], near, preferred_element_type=jnp.float32) * weight_of(b, slot)
 
@@ -315,9 +331,13 @@
         return carry
 
     lax.fori_loop(0, 4, side_features, 0)
-    for copy in o_copies:
+    await_row(halo, True, ext_o, o_send, o_recv)
+    lax.fori_loop(19, 25, sketch_pair, 0)
+    for copy in o_copies[3:5]:
         copy.wait_recv()
-    lax.fori_loop(19, 36, sketch_pair, 0)
+    lax.fori_loop(25, 30, sketch_pair, 0)
+    await_row(halo, False, ext_o, o_send, o_recv)
+    lax.fori_loop(30, 36, sketch_pair, 0)
 
     def add_units(b, carry):
         same = lax.broadcasted_iota(jnp.int32, (128, 128), 0) == lax.broadcasted_iota(jnp.int32, (128, 128), 1)
@@ -418,30 +438,39 @@
         return carry
 
     def couple_rest(i, carry):
-        couple_blocks([block_of(2 * i), block_of(2 * i + 1)], False)
+        couple_blocks([block_of(2 * i, own), block_of(2 * i + 1, own)], False)
         return carry
 
     lax.fori_loop(0, 4, couple_centres, 0)
     lax.fori_loop(0, 8, couple_pairs, 0)
-    for copy in b_copies + d_copies:
-        copy.wait_recv()
 
     def finish_near(r, c):
         near = ext_b[r, c]
         change = lax.dot_general(near, ext_d[r, c], NT, preferred_element_type=jnp.float32)
         ext_b[r, c] = (near.astype(jnp.float32) + change).astype(jnp.bfloat16)
 
-    def finish_across(t, carry):
-        finish_near(3 * (t // 6), t % 6)
-        return carry
+    def finish_row(row):
+        def finish(c, carry):
+            finish_near(row, c)
+            return carry
+
+        lax.fori_loop(0, TILE + 2, finish, 0)
 
     def finish_side(t, carry):
         finish_near(1 + t // 2, t % 2 * (TILE + 1))
         return carry
 
-    lax.fori_loop(0, 12, finish_across, 0)
+    await_row(halo, True, ext_b, b_send, b_recv)
+    await_row(halo, True, ext_d, d_send, d_recv)
+    for copy in b_copies[3:5] + d_copies[3:5]:
+        copy.wait_recv()
+    finish_row(3 * (1 - own))
     lax.fori_loop(0, 4, finish_side, 0)
-    lax.fori_loop(20, 36, couple_rest, 0)
+    lax.fori_loop(20, 30, couple_rest, 0)
+    await_row(halo, False, ext_b, b_send, b_recv)
+    await_row(halo, False, ext_d, d_send, d_recv)
+    finish_row(3 * own)
+    lax.fori_loop(30, 36, couple_rest, 0)
     keep, give = out_copies(slice(None), slice(None), own * 8, 8)
     keep.wait()
     give.wait()

time: 127 us -> 116 us (0.913)
  Pallas kernels: 117 us -> 106 us
    pallas_call x1, Pallas kernels: 117 us -> 106 us  [body(): pl.pallas_call(functools.partial(kernel, plate), out_shape=(jax.ShapeDtyp...]
where the time goes in v4:
time: 116 us
  Pallas kernels  106 us (91%)
  local copies, waits for them, and re-layouts  9.01 us (8%)
    pallas_call x1, Pallas kernels, body(): pl.pallas_call(functools.partial(kernel, plate), out_shape=(jax.ShapeDtyp...  106 us
    unnamed x3, local copies, waits for them, and re-layouts  9.01 us

profile of v4, /device:TPU:1, one launch (start us, length us, event | category | flops | bytes accessed | tf_op | source)
XLA Modules:
  0.0 116.1 jit_solution(4305967618571967145)
XLA Ops:
  0.6 1.5 %copy.5.points_ref = bf16[16,3,512]{2,1,0:T(4,128)(2,1)} copy(bf16[16,3,512]{2,0,1:T(8,128)(2,1)} %param.3) | data formatting | bytes 98304 | tf_op args[0]
  2.1 106.5 %plate_level.1 = (bf16[16,256,128]{2,1,0:T(8,128)(2,1)}, f32[16,9,64,128]{3,2,1,0:T(8,128)}) custom-call(s32[16,9]{1,0:T(8,128)} %mask_ref.1, bf16[16,3,512]{2,1,0:T(4,128)(2,1)} %copy.5.points_ref, bf16[16,256,128]{2,1,0:T(8,128)(2,1)} %sketch_ref.1), custom_call_target="tpu_custom_call" | custom-call | tf_op jit(solution)/shard_map/plate_level/pallas_call | solution.py:491
  108.6 2.3 %copy.8 = bf16[16,256,128]{2,1,0:T(8,128)(2,1)} copy(bf16[16,256,128]{2,1,0:T(8,128)(2,1)} %get-tuple-element.4) | data formatting | bytes 2097152
  110.9 5.2 %copy.9 = f32[16,9,64,128]{3,2,1,0:T(8,128)} copy(f32[16,9,64,128]{3,2,1,0:T(8,128)} %get-tuple-element.5) | data formatting | bytes 9437184

commit v5 on v4

--- a/solution.py
+++ b/solution.py
@@ -9,7 +9,6 @@
 from jax.sharding import PartitionSpec as P
 
 MESH = pl.DeviceIdType.MESH
-HIGHEST = lax.Precision.HIGHEST
 TILE = 4
 POINTS = 512
 RANK = 128
@@ -20,6 +19,10 @@
 PANEL = 16
 NT = (((1,), (1,)), ((), ()))
 TN = (((0,), (0,)), ((), ()))
+PAIRS = (
+    [[(c, 7) for c in range(4)]]
+    + [[(c, 5), (4 + c, 5), (c, 8), (c + 1, 6)] for c in range(3)]
+)
 DIRECTIONS = [(dy, dx) for dy in (-1, 0, 1) for dx in (-1, 0, 1) if (dy, dx) != (0, 0)]
 
 
@@ -171,12 +174,44 @@
     return r * TILE + c, 3 * (y + 1) + x + 1
 
 
-def pair_of(u):
-    below, down, back = (u + 10) // 16, (u + 6) // 16, (u + 3) // 16
-    r = u // 3 * (1 - below)
-    c = u % 3 * (1 - below) + (u - 6) * (below - down) + (u - 10) * (down - back) + (u - 12) * back
-    x = 1 - below + down - 2 * back
-    return r * TILE + c, 3 * (below + 1) + x + 1
+def full_gram(value):
+    a, b, c = parts(value, 3)
+    rank = value.shape[1]
+    wide = lax.dot_general(a, jnp.concatenate([a, b], 1), TN, preferred_element_type=jnp.float32)
+    rest = lax.dot_general(
+        jnp.concatenate([a, b], 0), jnp.concatenate([c, b * 0.5], 0), TN, preferred_element_type=jnp.float32
+    )
+    cross = wide[:, rank:] + rest
+    return wide[:, :rank] + (cross + cross.T)
+
+
+def full_apply(value, factor):
+    a, b, c = parts(value, 3)
+    p, q, r = parts(factor, 3)
+    rank = value.shape[1]
+    right = jnp.concatenate([jnp.concatenate([p, p], 1), jnp.concatenate([q, q], 1)], 0)
+    wide = lax.dot_general(jnp.concatenate([a, b], 1), right, NT, preferred_element_type=jnp.float32)
+    rest = lax.dot_general(
+        jnp.concatenate([c, a], 1), jnp.concatenate([p, r], 1), NT, preferred_element_type=jnp.float32
+    )
+    return wide[:, :rank] + (wide[:, rank:] + rest)
+
+
+def near_gram(value):
+    a, b = parts(value, 2)
+    rank = value.shape[1]
+    wide = lax.dot_general(a, jnp.concatenate([a, b], 1), TN, preferred_element_type=jnp.float32)
+    cross = wide[:, rank:]
+    return wide[:, :rank] + (cross + cross.T)
+
+
+def near_apply(value, factor):
+    a, b = parts(value, 2)
+    p, q = parts(factor, 2)
+    rank = value.shape[1]
+    right = jnp.concatenate([jnp.concatenate([p, p], 1), jnp.concatenate([q, jnp.zeros_like(q)], 1)], 0)
+    wide = lax.dot_general(jnp.concatenate([a, b], 1), right, NT, preferred_element_type=jnp.float32)
+    return wide[:, :rank] + wide[:, rank:]
 
 
 def kernel(
@@ -277,24 +312,29 @@
         fill_block(jnp.minimum(t + 2, 71), even)
         return carry
 
-    def couple_blocks(blocks, mirrored):
+    def couple_blocks(blocks, mirrored=False, batched=False):
         moved = []
         for b, slot in blocks:
             value = jnp.dot(basis_t[b], kbuf[b, slot], preferred_element_type=jnp.float32)
             moved.append(value.astype(jnp.bfloat16))
+        turned_blocks = []
         for (b, slot), value in zip(blocks, moved):
             y, x = slot // 3 - 1, slot % 3 - 1
             near = ext_b[b // TILE + 1 + y, b % TILE + 1 + x]
             value = jnp.dot(value, near, preferred_element_type=jnp.float32) * (1.0 / POINTS)
-            stage[b, slot] = value * weight_of(b, slot)
-            start_out(b, slot)
+            stage[b, slot] = (value * weight_of(b, slot)).astype(stage.dtype)
             if mirrored:
                 other_b = b + TILE * y + x
-                stage[other_b, 8 - slot] = value.T * weight_of(other_b, 8 - slot)
-                start_out(other_b, 8 - slot)
-
-    def start_out(b, slot):
-        keep, give = out_copies(pl.ds(b, 1), pl.ds(slot, 1), own * 8 + b, 1)
+                stage[other_b, 8 - slot] = (value.T * weight_of(other_b, 8 - slot)).astype(stage.dtype)
+                turned_blocks.append((other_b, 8 - slot))
+        for done in (blocks, turned_blocks):
+            if batched and done:
+                start_out(done[0][0], done[0][1], len(done))
+            for b, slot in [] if batched else done:
+                start_out(b, slot, 1)
+
+    def start_out(b, slot, count):
+        keep, give = out_copies(pl.ds(b, count), pl.ds(slot, 1), own * 8 + b, count)
         keep.start()
         give.start()
 
@@ -349,9 +389,17 @@
 
     lax.fori_loop(0, 8, add_units, 0)
 
+    def by_fours(step):
+        def four(i, carry):
+            for n in range(4):
+                step(4 * i + n, carry)
+            return carry
+
+        lax.fori_loop(0, 2, four, 0)
+
     def first_gram(b, carry):
         value = y_ref[b]
-        gram = lax.dot_general(value, value, TN, precision=HIGHEST, preferred_element_type=jnp.float32)
+        gram = full_gram(value)
         at = [lax.broadcasted_iota(jnp.int32, (RANK, RANK), axis) for axis in (0, 1)]
         diagonal = jnp.where(at[0] == at[1], gram, 0.0)
         along, across = [lax.rsqrt(jnp.sum(diagonal, axis=axis, keepdims=True)) for axis in (0, 1)]
@@ -360,33 +408,24 @@
         return carry
 
     def first_apply(b, carry):
-        value = lax.dot_general(
-            y_ref[b], p_ref[b] * scale_ref[b, 0:1], NT, precision=HIGHEST, preferred_element_type=jnp.float32
-        )
+        value = full_apply(y_ref[b], p_ref[b] * scale_ref[b, 0:1])
         work[b] = value
         rough[b // TILE, b % TILE] = value.astype(jnp.bfloat16)
         return carry
 
     def second_gram(b, carry):
-        high, low = parts(work[b], 2)
-        cross = lax.dot_general(high, low, TN, preferred_element_type=jnp.float32)
-        gram = lax.dot_general(high, high, TN, preferred_element_type=jnp.float32) + (cross + cross.T)
-        a_ref[b] = gram * (1.0 / POINTS)
+        a_ref[b] = near_gram(work[b]) * (1.0 / POINTS)
         return carry
 
     def second_apply(b, carry):
-        high, low = parts(work[b], 2)
-        p_high, p_low = parts(p_ref[b], 2)
-        value = lax.dot_general(high, p_high, NT, preferred_element_type=jnp.float32)
-        value += lax.dot_general(high, p_low, NT, preferred_element_type=jnp.float32)
-        value += lax.dot_general(low, p_high, NT, preferred_element_type=jnp.float32)
+        value = near_apply(work[b], p_ref[b])
         ext_b[1 + b // TILE, 1 + b % TILE] = value.astype(jnp.bfloat16)
         return carry
 
-    lax.fori_loop(0, 8, first_gram, 0)
+    by_fours(first_gram)
     eliminate(a_ref, p_ref, panel_ref)
-    lax.fori_loop(0, 8, first_apply, 0)
-    lax.fori_loop(0, 8, second_gram, 0)
+    by_fours(first_apply)
+    by_fours(second_gram)
     b_copies = halo.copies(rough, 0, ext_b, b_send, b_recv)
     for copy in b_copies:
         copy.start()
@@ -399,7 +438,7 @@
         return carry
 
     lax.fori_loop(0, 8, step_of, 0)
-    lax.fori_loop(0, 8, second_apply, 0)
+    by_fours(second_apply)
     d_copies = halo.copies(ext_d, 1, ext_d, d_send, d_recv)
     for copy in d_copies:
         copy.start()
@@ -430,19 +469,23 @@
         copy.start()
 
     def couple_centres(i, carry):
-        couple_blocks([(2 * i, 4), (2 * i + 1, 4)], False)
-        return carry
-
-    def couple_pairs(i, carry):
-        couple_blocks([pair_of(2 * i), pair_of(2 * i + 1)], True)
-        return carry
-
-    def couple_rest(i, carry):
-        couple_blocks([block_of(2 * i, own), block_of(2 * i + 1, own)], False)
-        return carry
-
-    lax.fori_loop(0, 4, couple_centres, 0)
-    lax.fori_loop(0, 8, couple_pairs, 0)
+        couple_blocks([(4 * i + n, 4) for n in range(4)], batched=True)
+        return carry
+
+    lax.fori_loop(0, 2, couple_centres, 0)
+    for n, pairs in enumerate(PAIRS):
+        couple_blocks(pairs, mirrored=True, batched=n == 0)
+
+    def couple_across(r, y):
+        def body(i, carry):
+            couple_blocks([(r * TILE + n, 3 * (y + 1) + i) for n in range(4)], batched=True)
+            return carry
+
+        lax.fori_loop(0, 3, body, 0)
+
+    def couple_sides(right, carry):
+        couple_blocks([(n // 2 * TILE + 3 * right, 3 * (n % 2 * (1 - n // 2 * 2) + 1) + 2 * right) for n in range(4)])
+        return carry
 
     def finish_near(r, c):
         near = ext_b[r, c]
@@ -466,11 +509,12 @@
         copy.wait_recv()
     finish_row(3 * (1 - own))
     lax.fori_loop(0, 4, finish_side, 0)
-    lax.fori_loop(20, 30, couple_rest, 0)
+    couple_across(1 - own, 1 - 2 * own)
+    lax.fori_loop(0, 2, couple_sides, 0)
     await_row(halo, False, ext_b, b_send, b_recv)
     await_row(halo, False, ext_d, d_send, d_recv)
     finish_row(3 * own)
-    lax.fori_loop(30, 36, couple_rest, 0)
+    couple_across(own, 2 * own - 1)
     keep, give = out_copies(slice(None), slice(None), own * 8, 8)
     keep.wait()
     give.wait()
@@ -488,11 +532,11 @@
     columns = pltpu.VMEM((4, TILE + 2, POINTS, RANK), jnp.bfloat16)
     tall = pltpu.VMEM((mine, POINTS, RANK), jnp.float32)
     square = pltpu.VMEM((mine, RANK, RANK), jnp.float32)
-    return pl.pallas_call(
+    basis, coupling = pl.pallas_call(
         functools.partial(kernel, plate),
         out_shape=(
             jax.ShapeDtypeStruct((boxes, POINTS // 2, RANK), jnp.bfloat16),
-            jax.ShapeDtypeStruct((boxes, SLOTS, RANK // 2, RANK), jnp.float32),
+            jax.ShapeDtypeStruct((boxes, SLOTS, RANK // 2, RANK), jnp.bfloat16),
         ),
         in_specs=[smem, hbm, hbm],
         out_specs=(hbm, hbm),
@@ -510,13 +554,14 @@
             pltpu.VMEM((PANEL, mine, RANK), jnp.float32),
             pltpu.VMEM((mine, 8, RANK), jnp.float32),
             pltpu.VMEM((mine, RANK, POINTS), jnp.bfloat16),
-            pltpu.VMEM((mine, SLOTS, RANK, RANK), jnp.float32),
+            pltpu.VMEM((mine, SLOTS, RANK, RANK), jnp.bfloat16),
             dma((4,)), dma, dma((2,)), dma((2,)), dma((8,)), dma((8,)), dma((8,)), dma((8,)),
             dma((8,)), dma((8,)), dma((8,)), dma((8,)), dma((2,)), dma((2,)), dma, dma,
         ],
         compiler_params=pltpu.CompilerParams(collective_id=0, has_side_effects=True, vmem_limit_bytes=LIMIT),
         name="plate_level",
     )(near_mask, points, sketch)
+    return basis, coupling.astype(jnp.float32)
 
 
 def solution(mesh):

time: 116 us -> 107 us (0.922)
  Pallas kernels: 106 us -> 98.9 us
  local copies, waits for them, and re-layouts: 9.01 us -> 2.45 us
  other arithmetic: 0 us -> 4.47 us
    pallas_call x1, Pallas kernels: 106 us -> 98.9 us  [body(): pl.pallas_call(functools.partial(kernel, plate), out_shape=(jax.ShapeDtyp...]
    unnamed x3 -> x4, local copies, waits for them, and re-layouts: 9.01 us -> 2.45 us
    convert_element_type x0 -> x1, other arithmetic: none -> 4.47 us  [body(): return (basis, coupling.astype(jnp.float32))]
where the time goes in v5:
time: 107 us
  Pallas kernels  98.9 us (92%)
  other arithmetic  4.47 us (4%)
  local copies, waits for them, and re-layouts  2.45 us (2%)
    pallas_call x1, Pallas kernels, body(): pl.pallas_call(functools.partial(kernel, plate), out_shape=(jax.ShapeDtyp...  98.9 us
    convert_element_type x1, other arithmetic, body(): return (basis, coupling.astype(jnp.float32))  4.47 us
    unnamed x4, local copies, waits for them, and re-layouts  2.45 us

profile of v5, /device:TPU:1, one launch (start us, length us, event | category | flops | bytes accessed | tf_op | source)
XLA Modules:
  0.0 106.5 jit_solution(1163686192259723730)
XLA Ops:
  0.6 1.5 %copy.5.points_ref = bf16[16,3,512]{2,1,0:T(4,128)(2,1)} copy(bf16[16,3,512]{2,0,1:T(8,128)(2,1)} %param.3) | data formatting | bytes 98304 | tf_op args[0]
  2.1 98.9 %plate_level.1 = (bf16[16,256,128]{2,1,0:T(8,128)(2,1)}, bf16[16,9,64,128]{3,2,1,0:T(8,128)(2,1)}) custom-call(s32[16,9]{1,0:T(8,128)} %mask_ref.1, bf16[16,3,512]{2,1,0:T(4,128)(2,1)} %copy.5.points_ref, bf16[16,256,128]{2,1,0:T(8,128)(2,1)} %sketch_ref.1), custom_call_target="tpu_custom_call" | custom-call | tf_op jit(solution)/shard_map/plate_level/pallas_call | solution.py:535
  101.1 0.0 copy-start
  101.1 4.5 %convert_element_type.3 = f32[16,9,64,128]{3,2,1,0:T(8,128)} convert(bf16[16,9,64,128]{3,2,1,0:T(8,128)(2,1)} %get-tuple-element.5) | non-fusion elementwise | flops 1179648 | bytes 7077888 | tf_op jit(solution)/shard_map/convert_element_type | solution.py:564
  105.5 0.0 copy-done
  105.5 1.0 copy.7
Async XLA Ops:
  101.1 4.5 %copy-start = (bf16[16,256,128]{2,1,0:T(8,128)(2,1)S(1)}, bf16[16,256,128]{2,1,0:T(8,128)(2,1)}, u32[]{:S(2)}) copy-start(bf16[16,256,128]{2,1,0:T(8,128)(2,1)} %get-tuple-element.8) | copy-start | bytes 3145732

commit v6 on v5

--- a/solution.py
+++ b/solution.py
@@ -70,6 +70,25 @@
                 )
             )
         return made
+
+
+def row_copies(halo, near_core, own, ext, send, recv):
+    row = 1 - halo.col if near_core else halo.col
+    dy = 2 * row - 1
+    made = []
+    for dx in (-1, 0, 1):
+        n = 5 * row + dx + 1
+        made.append(
+            pltpu.make_async_remote_copy(
+                src_ref=own.at[row, {-1: 0, 0: slice(0, TILE), 1: TILE - 1}[dx]],
+                dst_ref=ext.at[3 * (1 - row), place(dx, TILE, TILE + 1, 0)],
+                send_sem=send.at[n],
+                recv_sem=recv.at[n],
+                device_id=halo.device(dy, dx),
+                device_id_type=MESH,
+            )
+        )
+    return made
 
 
 def await_row(halo, near_core, ext, send, recv):
@@ -387,7 +406,6 @@
             kbuf[b, 4, part, part] = (kbuf[b, 4, part, part].astype(jnp.float32) + unit).astype(jnp.bfloat16)
         return carry
 
-    lax.fori_loop(0, 8, add_units, 0)
 
     def by_fours(step):
         def four(i, carry):
@@ -424,11 +442,25 @@
 
     by_fours(first_gram)
     eliminate(a_ref, p_ref, panel_ref)
-    by_fours(first_apply)
+    b_copies = []
+    for near_core in (False, True):
+
+        def apply_row(n, carry, row=1 - own if near_core else own):
+            for m in range(2):
+                first_apply(row * TILE + 2 * n + m, carry)
+            return carry
+
+        lax.fori_loop(0, 2, apply_row, 0)
+        started = row_copies(halo, near_core, rough, ext_b, b_send, b_recv)
+        for copy in started:
+            copy.start()
+        b_copies += started
+    sides = halo.copies(rough, 0, ext_b, b_send, b_recv)[3:5]
+    for copy in sides:
+        copy.start()
+    b_copies += sides
+    lax.fori_loop(0, 8, add_units, 0)
     by_fours(second_gram)
-    b_copies = halo.copies(rough, 0, ext_b, b_send, b_recv)
-    for copy in b_copies:
-        copy.start()
     eliminate(a_ref, p_ref, panel_ref)
 
     def step_of(b, carry):
@@ -505,7 +537,7 @@
 
     await_row(halo, True, ext_b, b_send, b_recv)
     await_row(halo, True, ext_d, d_send, d_recv)
-    for copy in b_copies[3:5] + d_copies[3:5]:
+    for copy in sides + d_copies[3:5]:
         copy.wait_recv()
     finish_row(3 * (1 - own))
     lax.fori_loop(0, 4, finish_side, 0)

time: 107 us -> 106 us (level)
  no operation moved by 1% of the time
where the time goes in v6:
time: 106 us
  Pallas kernels  98 us (92%)
  other arithmetic  4.47 us (4%)
  local copies, waits for them, and re-layouts  2.45 us (2%)
    pallas_call x1, Pallas kernels, body(): pl.pallas_call(functools.partial(kernel, plate), out_shape=(jax.ShapeDtyp...  98 us
    convert_element_type x1, other arithmetic, body(): return (basis, coupling.astype(jnp.float32))  4.47 us
    unnamed x4, local copies, waits for them, and re-layouts  2.45 us

profile of v6, /device:TPU:1, one launch (start us, length us, event | category | flops | bytes accessed | tf_op | source)
XLA Modules:
  0.0 105.5 jit_solution(5088810059611140217)
XLA Ops:
  0.6 1.5 %copy.5.points_ref = bf16[16,3,512]{2,1,0:T(4,128)(2,1)} copy(bf16[16,3,512]{2,0,1:T(8,128)(2,1)} %param.3) | data formatting | bytes 98304 | tf_op args[0]
  2.1 98.0 %plate_level.1 = (bf16[16,256,128]{2,1,0:T(8,128)(2,1)}, bf16[16,9,64,128]{3,2,1,0:T(8,128)(2,1)}) custom-call(s32[16,9]{1,0:T(8,128)} %mask_ref.1, bf16[16,3,512]{2,1,0:T(4,128)(2,1)} %copy.5.points_ref, bf16[16,256,128]{2,1,0:T(8,128)(2,1)} %sketch_ref.1), custom_call_target="tpu_custom_call" | custom-call | tf_op jit(solution)/shard_map/plate_level/pallas_call | solution.py:567
  100.1 0.0 copy-start
  100.1 4.5 %convert_element_type.3 = f32[16,9,64,128]{3,2,1,0:T(8,128)} convert(bf16[16,9,64,128]{3,2,1,0:T(8,128)(2,1)} %get-tuple-element.5) | non-fusion elementwise | flops 1179648 | bytes 7077888 | tf_op jit(solution)/shard_map/convert_element_type | solution.py:596
  104.6 0.0 copy-done
  104.6 1.0 copy.7
Async XLA Ops:
  100.1 4.5 %copy-start = (bf16[16,256,128]{2,1,0:T(8,128)(2,1)S(1)}, bf16[16,256,128]{2,1,0:T(8,128)(2,1)}, u32[]{:S(2)}) copy-start(bf16[16,256,128]{2,1,0:T(8,128)(2,1)} %get-tuple-element.8) | copy-start | bytes 3145732
